TPU v7x, 32 devices: a whole 2x2x4 slice. The times are simulated.
32 devices in a mesh: ctx: 8 (over y, x, core), head: 4 (over z).
Axes of the slice: x: 2, y: 2, z: 4, core: 2. Of those that a mesh axis runs over, the one named last changes fastest.
Arguments:
- queries: bfloat16 [2048, 4096], P('ctx', 'head'), may hold values from -6 to 6
- key_rows: bfloat16 [2048, 4096], P('ctx', 'head'), may hold values from -6 to 6
- value_rows: bfloat16 [2048, 4096], P('ctx', 'head'), may hold values from -6 to 6
- out_weight: bfloat16 [4096, 4096], P('head'), may hold values from -0.125 to 0.125
- cotangent: bfloat16 [2048, 4096], P('ctx', 'head'), may hold values from -6 to 6
Outputs:
- mixed: bfloat16 [2048, 4096], P('ctx', 'head')
- grad_queries: bfloat16 [2048, 4096], P('ctx', 'head')
- grad_keys: bfloat16 [2048, 4096], P('ctx', 'head')
- grad_values: bfloat16 [2048, 4096], P('ctx', 'head')
- grad_out_weight: float32 [4096, 4096], P('head', 'ctx')
All inputs are finite; a program needn't handle non-finite values.
Results may differ from a plain program's by a relative error of at most 0.0052.
Values may be sent and summed in bfloat16 or wider, within the bound.
No kernel may reach another device: no remote copies, remote signals or barrier semaphores. Data moves between devices by JAX's collectives and lax.ppermute only.
A program may use at most 64 MiB of HBM per device.

v0:
```python
import functools

import jax
import jax.numpy as jnp
from jax import lax
from jax.experimental import pallas as pl
from jax.experimental.pallas import tpu as pltpu
from jax.sharding import PartitionSpec as P


HEAD_DIM = 128

epsilon = 1e-06


bf16 = jnp.bfloat16
f32 = jnp.float32
VMEM = pl.BlockSpec(memory_space=pltpu.VMEM)
GRANT = 12 << 20


def mm(a, b, da, db):
    return lax.dot_general(a, b, (((da,), (db,)), ((), ())), preferred_element_type=f32)


def split(x):
    high = x.astype(bf16)
    return high, (x - high.astype(f32)).astype(bf16)


def head(h):
    return slice(h * HEAD_DIM, (h + 1) * HEAD_DIM)


def below(n):
    return lax.broadcasted_iota(jnp.int32, (n, n), 0) >= lax.broadcasted_iota(jnp.int32, (n, n), 1)


def array(shape, dtype):
    return jax.ShapeDtypeStruct(shape, dtype)


def kernel_call(kernel, *args, **settings):
    return pl.pallas_call(kernel, compiler_params=pltpu.CompilerParams(vmem_limit_bytes=GRANT), **settings)(*args)


def call(kernel, outs, *args):
    return kernel_call(
        kernel, *args, out_shape=outs, in_specs=[VMEM] * len(args), out_specs=jax.tree.map(lambda _: VMEM, outs)
    )


def state_kernel(k_far, v_far, out, k, v, sems):
    chunks = sems.shape[1]
    rows = k.shape[0] // chunks
    copies = []
    for n, (far, near) in enumerate(((k_far, k), (v_far, v))):
        for c in range(chunks):
            cut = pl.ds(c * rows, rows)
            copies.append(pltpu.make_async_copy(far.at[cut, :], near.at[cut, :], sems.at[n, c]))
            copies[-1].start()
    for copy in copies:
        copy.wait()
    for h in range(k.shape[1] // HEAD_DIM):
        out[head(h), :] = mm(k[:, head(h)], v[:, head(h)], 0, 0)


def intra_kernel(q, k, v, out):
    keep = below(q.shape[0])
    for h in range(q.shape[1] // HEAD_DIM):
        scores = jnp.where(keep, mm(q[:, head(h)], k[:, head(h)], 1, 1), 0.0).astype(bf16)
        out[:, head(h)] = mm(scores, v[:, head(h)], 1, 0)


def counts_at(at, mask, upward):
    return lax.rem(lax.div(at[1], mask), 2) == (1 if upward else 0)


def half_at(at, flip, rows):
    core = lax.rem(at[1], 2)
    return pl.ds(pl.multiple_of((1 - core if flip else core) * rows, rows), rows)


def core_step_kernel(upward, at, block, other, outer, *outs):
    outer[...] = jnp.zeros_like(outer)

    @pl.when(counts_at(at, 1, upward))
    def _():
        outer[...] = other[...]

    if outs:
        mine = half_at(at, False, outs[0].shape[0])
        total = block[mine, :] + other[mine, :]
        outs[0][...] = total.astype(bf16)
        for out in outs[1:]:
            out[...] = total


def chips_kernel(masks, upward, at, *refs):
    others, out = refs[:-1], refs[-1]
    out[...] = jnp.zeros_like(out)
    for mask, other in zip(masks, others):

        @pl.when(counts_at(at, 1 << (mask.bit_length() - 1), upward))
        def _(other=other):
            out[...] += other[...].astype(f32)


def step_kernel(mask, upward, fresh, last, at, total, *refs):
    outer, other, outs = None if fresh else refs[0], refs[0 if fresh else 1], refs[1 if fresh else 2 :]
    value = other[...].astype(f32)
    outs[0][...] = jnp.zeros_like(value) if fresh else outer[...]

    @pl.when(counts_at(at, mask, upward))
    def _():
        outs[0][...] += value

    if not last:
        whole = total[...] + value
        outs[1][...] = whole
        outs[2][...] = whole.astype(bf16)


def join_kernel(at, outer, mine, theirs, out):
    rows = mine.shape[0]
    here, there = half_at(at, False, rows), half_at(at, True, rows)
    out[here, :] = outer[here, :] + mine[...]
    out[there, :] = outer[there, :] + theirs[...]


def row_scale_of(attended):
    return lax.rsqrt(jnp.mean(attended * attended, axis=-1, keepdims=True) + epsilon)


def norm_kernel(q, intra, prefix, attended, normed):
    for h in range(q.shape[1] // HEAD_DIM):
        high, low = split(prefix[head(h), :])
        query = q[:, head(h)]
        value = intra[:, head(h)] + mm(query, high, 1, 0) + mm(query, low, 1, 0)
        attended[:, head(h)] = value
        normed[:, head(h)] = (value * row_scale_of(value)).astype(bf16)


def block_at(ref, block, width):
    return ref[:, pl.ds(pl.multiple_of(block * width, width), width)]


def piece_kernel(block_of, at, weight, normed, *refs):
    extras, out = refs[:-1], refs[-1]
    value = mm(normed[...], block_at(weight, block_of(at[0]), out.shape[1]), 1, 0)
    for ref in extras:
        value = value + ref[...].astype(f32)
    out[...] = value.astype(bf16)


def far_piece_kernel(block_of, at, weight, normed, out, buffer, sems):
    chunks, rows, part = buffer.shape
    columns = pl.ds(pl.multiple_of(block_of(at[0]) * part, part), part)
    copies = []
    for c in range(chunks):
        source = weight.at[pl.ds(c * rows, rows), columns]
        copies.append(pltpu.make_async_copy(source, buffer.at[c], sems.at[c]))
        copies[-1].start()
    value = None
    for c, copy in enumerate(copies):
        copy.wait()
        term = mm(normed[:, c * rows : (c + 1) * rows], buffer[c], 1, 0)
        value = term if value is None else value + term
    out[...] = value.astype(bf16)


def add_terms(out, place, blocks, sources, weight):
    for ref, source in zip(blocks, sources):
        block, valid = source(place)

        @pl.when(valid)
        def _(ref=ref, block=block):
            out[...] += mm(ref[...], block_at(weight, block, ref.shape[1]), 1, 1)


def upstream_kernel(own, sources, at, weight, first, *refs):
    blocks, out = refs[:-1], refs[-1]
    if own:
        out[...] = mm(first[...], block_at(weight, at[0], first.shape[1]), 1, 1)
    else:
        out[...] = first[...]
    add_terms(out, at[0], blocks, sources, weight)


def finish_kernel(sources, at, weight, so_far, attended, q, *refs):
    blocks, (d_out, grad_out, upstream) = refs[:-3], refs[-3:]
    upstream[...] = so_far[...]
    add_terms(upstream, at[0], blocks, sources, weight)
    for h in range(d_out.shape[1] // HEAD_DIM):
        value, up = attended[:, head(h)], upstream[:, head(h)]
        scale = row_scale_of(value)
        unit = value * scale
        grad = scale * (up - unit * jnp.mean(up * unit, axis=-1, keepdims=True))
        grad = grad.astype(bf16)
        d_out[:, head(h)] = grad
        grad_out[head(h), :] = mm(q[:, head(h)], grad, 0, 0)


def pick_kernel(choices, at, *refs):
    sources, outs = refs[: len(refs) - len(choices)], refs[len(refs) - len(choices) :]
    for choice, out in zip(choices, outs):
        chosen = choice(at[0], at[1])
        for m, source in enumerate(sources):

            @pl.when(chosen == m)
            def _(out=out, source=source):
                out[...] = source[...]


def back_kernel(q, k, v, d, prefix, grad_q, part_k, part_v):
    keep = below(q.shape[0])
    for h in range(q.shape[1] // HEAD_DIM):
        qh, kh, vh, dh = q[:, head(h)], k[:, head(h)], v[:, head(h)], d[:, head(h)]
        high, low = split(prefix[head(h), :])
        scores = jnp.where(keep, mm(qh, kh, 1, 1), 0.0).astype(bf16)
        back = jnp.where(keep, mm(dh, vh, 1, 1), 0.0).astype(bf16)
        grad_q[:, head(h)] = (mm(back, kh, 1, 0) + mm(dh, high, 1, 1) + mm(dh, low, 1, 1)).astype(bf16)
        part_k[:, head(h)] = mm(back, qh, 0, 0)
        part_v[:, head(h)] = mm(scores, dh, 0, 0)


def suffix_kernel(k, v, part_k, part_v, suffix, grad_k, grad_v):
    for h in range(k.shape[1] // HEAD_DIM):
        high, low = split(suffix[head(h), :])
        kh, vh = k[:, head(h)], v[:, head(h)]
        grad_k[:, head(h)] = (part_k[:, head(h)] + mm(vh, high, 1, 1) + mm(vh, low, 1, 1)).astype(bf16)
        grad_v[:, head(h)] = (part_v[:, head(h)] + mm(kh, high, 1, 0) + mm(kh, low, 1, 0)).astype(bf16)


def weight_all_kernel(*refs):
    count = len(refs) // 2
    rows, cols, out = refs[:count], refs[count:-1], refs[-1]
    value = mm(rows[0][...], cols[0][...], 0, 0)
    for n in range(1, count):
        value = value + mm(rows[n][...], cols[n][...], 0, 0)
    out[...] = value


def weight_last_kernel(core_of, at, so_far, rows, cols, *refs):
    extras, out = refs[:-1], refs[-1]
    core, own_cols = core_of(at[1]), out.shape[1]
    value = block_at(so_far, core, own_cols) + mm(rows[...], block_at(cols, core, own_cols), 0, 0)
    for ref in extras:
        value = value + ref[...].astype(f32)
    out[...] = value.astype(out.dtype)


def flipped(size, mask):
    return [(i, i ^ mask) for i in range(size)]


def make_body(n_ctx, n_head):
    pair = min(2, n_ctx)
    chips = n_ctx // pair

    def body(queries, key_rows, value_rows, out_weight, cotangent):
        length, width = queries.shape
        model = out_weight.shape[1]
        part = model // n_head
        chip_cols = model // chips
        own_cols = chip_cols // pair
        position = lax.axis_index("ctx")
        place = lax.axis_index("head")
        wide = array((length, width), f32)
        narrow = array((length, width), bf16)
        piece = array((length, part), bf16)

        where = jnp.where(jnp.arange(2) == 0, place, position).astype(jnp.int32)

        def placed(kernel, outs, *args, scratch=(), far=0):
            args = [pltpu.with_memory_space_constraint(x, pltpu.HBM) for x in args[:far]] + list(args[far:])
            specs = [pl.BlockSpec(memory_space=pltpu.HBM)] * far + [VMEM] * (len(args) - far)
            return kernel_call(
                kernel,
                where,
                *args,
                out_shape=outs,
                in_specs=[pl.BlockSpec(memory_space=pltpu.SMEM)] + specs,
                out_specs=jax.tree.map(lambda _: VMEM, outs),
                scratch_shapes=scratch,
            )

        def exclusive_sum(block, upward):
            if n_ctx == 1:
                return jnp.zeros_like(block)
            rows = block.shape[0] // 2
            state, state_sent = array((rows, HEAD_DIM), f32), array((rows, HEAD_DIM), bf16)
            other = lax.ppermute(block, "ctx", flipped(n_ctx, 1))
            direct = chips <= 4
            outs = [array(block.shape, f32)]
            if chips > 1:
                outs += [state_sent] if direct else [state_sent, state]
            on_chip = placed(functools.partial(core_step_kernel, upward), outs, block, other)
            if chips == 1:
                return on_chip[0]
            if direct:
                on_chip, sent = on_chip
                masks, others = range(2, n_ctx, 2), []
                for mask in masks:
                    others.append(lax.ppermute(sent, "ctx", flipped(n_ctx, mask)))
                (mine,) = placed(functools.partial(chips_kernel, masks, upward), [state], *others)
                theirs = lax.ppermute(mine, "ctx", flipped(n_ctx, 1))
                return placed(join_kernel, array(block.shape, f32), on_chip, mine, theirs)
            on_chip, sent, total = on_chip
            outer, mask = [], 2
            while mask < n_ctx:
                other = lax.ppermute(sent, "ctx", flipped(n_ctx, mask))
                last = 2 * mask >= n_ctx
                summed = placed(
                    functools.partial(step_kernel, mask, upward, not outer, last),
                    [state] if last else [state, state, state_sent],
                    total,
                    *outer,
                    other,
                )
                outer = [summed[0]]
                if not last:
                    _, total, sent = summed
                mask *= 2
            theirs = lax.ppermute(outer[0], "ctx", flipped(n_ctx, 1))
            return placed(join_kernel, array(block.shape, f32), on_chip, outer[0], theirs)

        def line(r, p):
            over = []
            for link in range(p, n_head - 1, 2):
                if link - r + 1 >= 0:
                    over.append((link, link + 1))
                if link + r < n_head:
                    over.append((link + 1, link))
            return over

        def block_of(r, p, place):
            block = jnp.where(lax.rem(place, 2) == p, place + r, place - r)
            valid = (block >= 0) & (block < n_head)
            return jnp.minimum(jnp.maximum(block, 0), n_head - 1), valid

        rounds = [(r, p) for r in range(1, n_head) for p in range(2) if line(r, p)]
        got = {(0, 0): cotangent, (0, 1): cotangent}
        for r, p in rounds:
            if r < n_head - 1 or r == 1:
                got[r, p] = lax.ppermute(got[r - 1, 1 - p], "head", line(r, p))

        far = pl.BlockSpec(memory_space=pltpu.HBM)
        block_state = kernel_call(
            state_kernel,
            pltpu.with_memory_space_constraint(key_rows, pltpu.HBM),
            pltpu.with_memory_space_constraint(value_rows, pltpu.HBM),
            out_shape=array((width, HEAD_DIM), f32),
            in_specs=[far, far],
            out_specs=VMEM,
            scratch_shapes=[
                pltpu.VMEM((length, width), bf16),
                pltpu.VMEM((length, width), bf16),
                pltpu.SemaphoreType.DMA((2, 4 if length % 64 == 0 else 1)),
            ],
        )
        intra = call(intra_kernel, wide, queries, key_rows, value_rows)
        prefix = exclusive_sum(block_state, True)
        attended, normed = call(norm_kernel, (wide, narrow), queries, intra, prefix)

        def piece_of(name, block, *extras):
            if not extras and name == f"piece_{n_head - 1}_0":
                chunks = 4 if width % (4 * HEAD_DIM) == 0 else 1
                scratch = [
                    pltpu.VMEM((chunks, width // chunks, part), bf16),
                    pltpu.SemaphoreType.DMA((chunks,)),
                ]
                kernel = functools.partial(far_piece_kernel, block)
                return placed(kernel, piece, out_weight, normed, scratch=scratch, far=1)
            kernel = functools.partial(piece_kernel, block)
            return placed(kernel, piece, out_weight, normed, *extras)

        came = {}
        for r, p in sorted(rounds, key=lambda at: -at[0]):
            extras = [came[r + 1, 1 - p]] if (r + 1, 1 - p) in came else []
            sent = piece_of(f"piece_{r}_{p}", lambda i, r=r, p=p: block_of(r, p, i)[0], *extras)
            back = [(j, i) for i, j in line(r, p)]
            if (r, p) in got:
                came[r, p] = lax.ppermute(sent, "head", back)
            else:
                ends = [i for i, _ in back]

                def gives(place, position, ends=ends):
                    return functools.reduce(jnp.logical_or, [place == i for i in ends]).astype(jnp.int32)

                (sent,) = placed(functools.partial(pick_kernel, [gives]), [piece], got[r - 1, 1 - p], sent)
                got[r, p] = came[r, p] = lax.ppermute(sent, "head", line(r, p) + back)
        mixed = piece_of("piece_last", lambda i: i, *[came[at] for at in ((1, 0), (1, 1)) if at in came])

        masks = list(range(pair, n_ctx, pair))
        rows_by = {0: normed}
        for mask in masks:
            low = mask & -mask
            high = mask ^ low
            if high == 0 or pair == 1:
                sent, via = normed, flipped(n_ctx, mask)
            else:
                (sent,) = placed(
                    functools.partial(pick_kernel, [lambda place, position: lax.rem(position, pair)]),
                    [narrow],
                    rows_by[high],
                    rows_by[low],
                )
                via = [(i, i ^ (low if i % pair == 0 else high)) for i in range(n_ctx)]
            rows_by[mask] = lax.ppermute(sent, "ctx", via)
        rows = [rows_by[mask] for mask in [0] + masks]

        def sources_of(here):
            return [functools.partial(block_of, *at) for at in here]

        upstream = placed(functools.partial(upstream_kernel, True, []), wide, out_weight, cotangent)
        for r in range(1, n_head - 1):
            here = [at for at in rounds if at[0] == r]
            upstream = placed(
                functools.partial(upstream_kernel, False, sources_of(here)),
                wide,
                out_weight,
                upstream,
                *[got[at] for at in here],
            )
        here = [at for at in rounds if at[0] == n_head - 1]
        d_attended, grad_block = placed(
            functools.partial(finish_kernel, sources_of(here)),
            (narrow, array((width, HEAD_DIM), f32)),
            out_weight,
            upstream,
            attended,
            queries,
            *[got[at] for at in here],
            scratch=[pltpu.VMEM((length, width), f32)],
        )

        if chip_cols == part:

            def choice_of(mask, place, position):
                target = lax.div(position ^ mask, pair)
                chosen = jnp.int32(0)
                for n, at in enumerate(rounds):
                    block, valid = block_of(*at, place)
                    chosen = jnp.where(valid & (block == target), n + 1, chosen)
                return chosen

            cols = placed(
                functools.partial(pick_kernel, [functools.partial(choice_of, mask) for mask in [0] + masks]),
                [piece] * chips,
                cotangent,
                *[got[at] for at in rounds],
            )
        else:
            whole = jnp.zeros((n_head, length, part), bf16)
            whole = lax.dynamic_update_index_in_dim(whole, cotangent, place, 0)
            for at in rounds:
                block, valid = block_of(*at, place)
                old = lax.dynamic_index_in_dim(whole, block, 0, keepdims=False)
                whole = lax.dynamic_update_index_in_dim(whole, jnp.where(valid, got[at], old), block, 0)
            whole = whole.transpose(1, 0, 2).reshape(length, model)
            starts = [lax.div(position ^ mask, pair) * chip_cols for mask in [0] + masks]
            cols = [lax.dynamic_slice(whole, (0, start), (length, chip_cols)) for start in starts]
        cols = list(cols)
        for n, mask in enumerate(masks):
            cols[n + 1] = lax.ppermute(cols[n + 1], "ctx", flipped(n_ctx, mask))

        grad_q, part_k, part_v = call(
            back_kernel, (narrow, wide, wide), queries, key_rows, value_rows, d_attended, prefix
        )
        suffix = exclusive_sum(grad_block, False)
        grad_k, grad_v = call(suffix_kernel, (narrow, narrow), key_rows, value_rows, part_k, part_v, suffix)

        def same(position):
            return lax.rem(position, pair)

        def partner(position):
            return 1 - lax.rem(position, pair)

        if chips > 1:
            whole = array((width, chip_cols), f32)
            so_far = call(weight_all_kernel, whole, *rows[:-1], *cols[:-1])
        else:
            so_far = jnp.zeros((width, chip_cols), f32)

        def weight_last(core_of, dtype, *extra):
            kernel = functools.partial(weight_last_kernel, core_of)
            return placed(kernel, array((width, own_cols), dtype), so_far, rows[-1], cols[-1], *extra)

        extra = []
        if pair > 1:
            other = weight_last(partner, bf16)
            extra = [lax.ppermute(other, "ctx", flipped(n_ctx, 1))]
        grad_out_weight = weight_last(same, f32, *extra)
        return mixed, grad_q, grad_k, grad_v, grad_out_weight

    return body


def solution(mesh):
    n_ctx, n_head = mesh.shape["ctx"], mesh.shape["head"]
    body = make_body(n_ctx, n_head)

    return jax.shard_map(
        body,
        mesh=mesh,
        in_specs=(P("ctx", "head"),) * 3 + (P("head", None), P("ctx", "head")),
        out_specs=(P("ctx", "head"),) * 4 + (P("head", "ctx"),),
        check_vma=False,
    )
```

profile of v0, /device:TPU:0, one launch (start us, length us, event | category | flops | bytes accessed | tf_op | source)
XLA Modules:
  0.0 117.4 jit_solution(656355913734482642)
XLA Ops:
  0.6 3.1 %collective-permute-start.5 = (bf16[256,1024]{1,0:T(8,128)(2,1)}, bf16[256,1024]{1,0:T(8,128)(2,1)S(1)}, u32[]{:S(2)}, u32[]{:S(2)}) collective-permute-start(bf16[256,1024]{1,0:T(8,128)(2,1)} %refs_0_.1), channel_id=1, source_target_pairs={{0,1},{1,0},{2,3},{3,2},{4,5},{5,4},{6,7},{7,6},{8,9},{9,8},{10,11... | collective-permute-start | bytes 1572872 | tf_op jit(solution)/shard_map/ppermute | solution.py:346
  3.8 1.7 %shard_map.93.block = f32[1024,128]{1,0:T(8,128)S(1)} custom-call(bf16[256,1024]{1,0:T(8,128)(2,1)} %k.5, bf16[256,1024]{1,0:T(8,128)(2,1)} %v.5), custom_call_target="tpu_custom_call" | custom-call | tf_op jit(solution)/shard_map/pallas_call | solution.py:44
  6.3 9.6 %collective-permute-done.5.refs_0_.refs_1_ = bf16[256,1024]{1,0:T(8,128)(2,1)S(1)} collective-permute-done((bf16[256,1024]{1,0:T(8,128)(2,1)}, bf16[256,1024]{1,0:T(8,128)(2,1)S(1)}, u32[]{:S(2)}, u32[]{:S(2)}) %collective-permute-start.5) | collective-permute-done | bytes 524320 | tf_op jit(solution)/shard_map/ppermute | solution.py:346
  17.2 2.7 %collective-permute-start.3 = (bf16[512,128]{1,0:T(8,128)(2,1)S(1)}, bf16[512,128]{1,0:T(8,128)(2,1)S(1)}, u32[]{:S(2)}, u32[]{:S(2)}) collective-permute-start(bf16[512,128]{1,0:T(8,128)(2,1)S(1)} %get-tuple-element.23), channel_id=1, source_target_pairs={{0,24},{4,28},{8,16},{12,20},{16,8},{20,12},{24,0},{28,4},{1,25},{... | collective-permute-start | bytes 393224 | tf_op jit(solution)/shard_map/ppermute | solution.py:305
  20.8 3.1 %collective-permute-done.3.refs_2_ = bf16[512,128]{1,0:T(8,128)(2,1)S(1)} collective-permute-done((bf16[512,128]{1,0:T(8,128)(2,1)S(1)}, bf16[512,128]{1,0:T(8,128)(2,1)S(1)}, u32[]{:S(2)}, u32[]{:S(2)}) %collective-permute-start.3) | collective-permute-done | bytes 131104 | tf_op jit(solution)/shard_map/ppermute | solution.py:305
  23.9 1.8 %collective-permute-done.2.refs_1_ = bf16[512,128]{1,0:T(8,128)(2,1)S(1)} collective-permute-done((bf16[512,128]{1,0:T(8,128)(2,1)S(1)}, bf16[512,128]{1,0:T(8,128)(2,1)S(1)}, u32[]{:S(2)}, u32[]{:S(2)}) %collective-permute-start.2) | collective-permute-done | bytes 131104 | tf_op jit(solution)/shard_map/ppermute | solution.py:305
  30.4 1.3 %collective-permute-start.13 = (bf16[256,1024]{1,0:T(8,128)(2,1)S(1)}, bf16[256,1024]{1,0:T(8,128)(2,1)S(1)}, u32[]{:S(2)}, u32[]{:S(2)}) collective-permute-start(bf16[256,1024]{1,0:T(8,128)(2,1)S(1)} %collective-permute-done.12.refs_1_.refs_2_), channel_id=1, source_target_pairs={{1,0},{2,3},{5,4},{6,7},{9,8},{10,11},{13,12},{14,15},{17,16},{18,... | collective-permute-start | bytes 1572872 | tf_op jit(solution)/shard_map/ppermute | solution.py:346
  33.0 2.9 %shard_map.98.refs_1_ = bf16[256,1024]{1,0:T(8,128)(2,1)S(1)} custom-call(s32[2]{0:T(128)S(1)} %compare_select_fusion.at, bf16[1024,4096]{1,0:T(8,128)(2,1)} %weight.19, bf16[256,1024]{1,0:T(8,128)(2,1)S(1)} %get-tuple-element.24.normed.refs_0_), custom_call_target="tpu_custom_call" | custom-call | tf_op jit(solution)/shard_map/pallas_call | solution.py:44
  36.5 4.2 %collective-permute-start.7 = (bf16[256,1024]{1,0:T(8,128)(2,1)S(1)}, bf16[256,1024]{1,0:T(8,128)(2,1)S(1)}, u32[]{:S(2)}, u32[]{:S(2)}) collective-permute-start(bf16[256,1024]{1,0:T(8,128)(2,1)S(1)} %shard_map.99), channel_id=1, source_target_pairs={{1,0},{2,3},{0,1},{3,2},{5,4},{6,7},{4,5},{7,6},{9,8},{10,11},{8,9... | collective-permute-start | bytes 1572872 | tf_op jit(solution)/shard_map/ppermute | solution.py:392
  40.6 1.5 %collective-permute-start.20 = (bf16[256,1024]{1,0:T(8,128)(2,1)S(1)}, bf16[256,1024]{1,0:T(8,128)(2,1)S(1)}, u32[]{:S(2)}, u32[]{:S(2)}) collective-permute-start(bf16[256,1024]{1,0:T(8,128)(2,1)S(1)} %get-tuple-element.24.normed.refs_0_), channel_id=1, source_target_pairs={{0,16},{4,20},{8,24},{12,28},{16,0},{20,4},{24,8},{28,12},{1,17},{... | collective-permute-start | bytes 1572872 | tf_op jit(solution)/shard_map/ppermute | solution.py:410
  42.9 5.6 %collective-permute-done.13.refs_0_.refs_3_ = bf16[256,1024]{1,0:T(8,128)(2,1)S(1)} collective-permute-done((bf16[256,1024]{1,0:T(8,128)(2,1)S(1)}, bf16[256,1024]{1,0:T(8,128)(2,1)S(1)}, u32[]{:S(2)}, u32[]{:S(2)}) %collective-permute-start.13) | collective-permute-done | bytes 524320 | tf_op jit(solution)/shard_map/ppermute | solution.py:346
  48.6 11.0 %collective-permute-done.7.refs_0_.refs_5_ = bf16[256,1024]{1,0:T(8,128)(2,1)S(1)} collective-permute-done((bf16[256,1024]{1,0:T(8,128)(2,1)S(1)}, bf16[256,1024]{1,0:T(8,128)(2,1)S(1)}, u32[]{:S(2)}, u32[]{:S(2)}) %collective-permute-start.7) | collective-permute-done | bytes 524320 | tf_op jit(solution)/shard_map/ppermute | solution.py:392
  60.5 1.6 %collective-permute-start.21 = (bf16[256,1024]{1,0:T(8,128)(2,1)S(1)}, bf16[256,1024]{1,0:T(8,128)(2,1)S(1)}, u32[]{:S(2)}, u32[]{:S(2)}) collective-permute-start(bf16[256,1024]{1,0:T(8,128)(2,1)S(1)} %get-tuple-element.36), channel_id=1, source_target_pairs={{0,8},{4,12},{8,0},{12,4},{16,24},{20,28},{24,16},{28,20},{1,9},{5... | collective-permute-start | bytes 1572872 | tf_op jit(solution)/shard_map/ppermute | solution.py:466
  63.4 1.4 %collective-permute-start.23 = (bf16[256,1024]{1,0:T(8,128)(2,1)S(1)}, bf16[256,1024]{1,0:T(8,128)(2,1)S(1)}, u32[]{:S(2)}, u32[]{:S(2)}) collective-permute-start(bf16[256,1024]{1,0:T(8,128)(2,1)S(1)} %shard_map.116), channel_id=1, source_target_pairs={{0,8},{4,20},{8,0},{12,28},{16,24},{20,4},{24,16},{28,12},{1,9},{5... | collective-permute-start | bytes 1572872 | tf_op jit(solution)/shard_map/ppermute | solution.py:410
  64.8 1.4 %collective-permute-start.24 = (bf16[256,1024]{1,0:T(8,128)(2,1)S(1)}, bf16[256,1024]{1,0:T(8,128)(2,1)S(1)}, u32[]{:S(2)}, u32[]{:S(2)}) collective-permute-start(bf16[256,1024]{1,0:T(8,128)(2,1)S(1)} %get-tuple-element.38), channel_id=1, source_target_pairs={{0,24},{4,28},{8,16},{12,20},{16,8},{20,12},{24,0},{28,4},{1,25},{... | collective-permute-start | bytes 1572872 | tf_op jit(solution)/shard_map/ppermute | solution.py:466
  66.2 1.3 %shard_map.105.first = f32[256,1024]{1,0:T(8,128)S(1)} custom-call(s32[2]{0:T(128)S(1)} %compare_select_fusion.at, bf16[1024,4096]{1,0:T(8,128)(2,1)S(1)} %bitcast.1, bf16[256,1024]{1,0:T(8,128)(2,1)S(1)} %copy-done.6), custom_call_target="tpu_custom_call" | custom-call | tf_op jit(solution)/shard_map/pallas_call | solution.py:44
  67.5 1.4 %shard_map.106.first = f32[256,1024]{1,0:T(8,128)S(1)} custom-call(s32[2]{0:T(128)S(1)} %compare_select_fusion.at, bf16[1024,4096]{1,0:T(8,128)(2,1)S(1)} %bitcast.1, f32[256,1024]{1,0:T(8,128)S(1)} %shard_map.105.first, bf16[256,1024]{1,0:T(8,128)(2,1)S(1)} %collective-permute-done.5.refs_0_.refs_1_, ...), custom_call_target="tpu_custom_call" | custom-call | tf_op jit(solution)/shard_map/pallas_call | solution.py:44
  68.9 1.4 %shard_map.107.so_far = f32[256,1024]{1,0:T(8,128)S(1)} custom-call(s32[2]{0:T(128)S(1)} %compare_select_fusion.at, bf16[1024,4096]{1,0:T(8,128)(2,1)S(1)} %bitcast.1, f32[256,1024]{1,0:T(8,128)S(1)} %shard_map.106.first, bf16[256,1024]{1,0:T(8,128)(2,1)S(1)} %collective-permute-done.13.refs_0_.refs_3_, ...), custom_call_target="tpu_custom_call" | custom-call | tf_op jit(solution)/shard_map/pallas_call | solution.py:44
  70.3 2.6 %shard_map.108 = (bf16[256,1024]{1,0:T(8,128)(2,1)S(1)}, f32[1024,128]{1,0:T(8,128)S(1)}) custom-call(s32[2]{0:T(128)S(1)} %compare_select_fusion.at, bf16[1024,4096]{1,0:T(8,128)(2,1)S(1)} %bitcast.1, f32[256,1024]{1,0:T(8,128)S(1)} %shard_map.107.so_far, f32[256,1024]{1,0:T(8,128)S(1)} %get-tuple-element.25.attended, bf16[256,1024]{1,0:T(8,128)(2,1)S(1)} %copy-done.5, ...), custom_call_target="tpu_custom_call" | custom-call | tf_op jit(solution)/shard_map/pallas_call | solution.py:44
  75.5 1.5 %collective-permute-start.10 = (bf16[256,1024]{1,0:T(8,128)(2,1)S(1)}, bf16[256,1024]{1,0:T(8,128)(2,1)S(1)}, u32[]{:S(2)}, u32[]{:S(2)}) collective-permute-start(bf16[256,1024]{1,0:T(8,128)(2,1)S(1)} %shard_map.102), channel_id=1, source_target_pairs={{0,1},{3,2},{4,5},{7,6},{8,9},{11,10},{12,13},{15,14},{16,17},{19,... | collective-permute-start | bytes 1572872 | tf_op jit(solution)/shard_map/ppermute | solution.py:384
  77.0 2.5 %collective-permute-done.22.refs_5_ = bf16[256,1024]{1,0:T(8,128)(2,1)S(1)} collective-permute-done((bf16[256,1024]{1,0:T(8,128)(2,1)S(1)}, bf16[256,1024]{1,0:T(8,128)(2,1)S(1)}, u32[]{:S(2)}, u32[]{:S(2)}) %collective-permute-start.22) | collective-permute-done | bytes 524320 | tf_op jit(solution)/shard_map/ppermute | solution.py:466
  80.4 1.8 %shard_map.115.so_far = f32[1024,1024]{1,0:T(8,128)S(1)} custom-call(bf16[256,1024]{1,0:T(8,128)(2,1)S(1)} %get-tuple-element.24.normed.refs_0_, bf16[256,1024]{1,0:T(8,128)(2,1)S(1)} %collective-permute-done.19.refs_1_, bf16[256,1024]{1,0:T(8,128)(2,1)S(1)} %collective-permute-done.20.refs_2_.refs_0_, bf16[256,1024]{1,0:T(8,128)(2,1)S(1)} %get-tuple-element.35.refs_3_, ...), custom_call_target="tpu_custom_call" | custom-call | tf_op jit(solution)/shard_map/pallas_call | solution.py:44
  82.2 3.3 %collective-permute-done.23.rows = bf16[256,1024]{1,0:T(8,128)(2,1)S(1)} collective-permute-done((bf16[256,1024]{1,0:T(8,128)(2,1)S(1)}, bf16[256,1024]{1,0:T(8,128)(2,1)S(1)}, u32[]{:S(2)}, u32[]{:S(2)}) %collective-permute-start.23) | collective-permute-done | bytes 524320 | tf_op jit(solution)/shard_map/ppermute | solution.py:410
  85.5 6.7 %collective-permute-done.24.cols = bf16[256,1024]{1,0:T(8,128)(2,1)S(1)} collective-permute-done((bf16[256,1024]{1,0:T(8,128)(2,1)S(1)}, bf16[256,1024]{1,0:T(8,128)(2,1)S(1)}, u32[]{:S(2)}, u32[]{:S(2)}) %collective-permute-start.24) | collective-permute-done | bytes 524320 | tf_op jit(solution)/shard_map/ppermute | solution.py:466
  94.0 1.5 %collective-permute-start.17 = (bf16[512,128]{1,0:T(8,128)(2,1)S(1)}, bf16[512,128]{1,0:T(8,128)(2,1)S(1)}, u32[]{:S(2)}, u32[]{:S(2)}) collective-permute-start(bf16[512,128]{1,0:T(8,128)(2,1)S(1)} %get-tuple-element.32), channel_id=1, source_target_pairs={{0,24},{4,28},{8,16},{12,20},{16,8},{20,12},{24,0},{28,4},{1,25},{... | collective-permute-start | bytes 393224 | tf_op jit(solution)/shard_map/ppermute | solution.py:305
  99.0 1.7 %collective-permute-start.9 = (bf16[256,1024]{1,0:T(8,128)(2,1)S(1)}, bf16[256,1024]{1,0:T(8,128)(2,1)S(1)}, u32[]{:S(2)}, u32[]{:S(2)}) collective-permute-start(bf16[256,1024]{1,0:T(8,128)(2,1)S(1)} %shard_map.101), channel_id=1, source_target_pairs={{1,0},{0,1},{3,2},{2,3},{5,4},{4,5},{7,6},{6,7},{9,8},{8,9},{11,10... | collective-permute-start | bytes 1572872 | tf_op jit(solution)/shard_map/ppermute | solution.py:384
  101.1 1.6 %collective-permute-start.15 = (bf16[512,128]{1,0:T(8,128)(2,1)S(1)}, bf16[512,128]{1,0:T(8,128)(2,1)S(1)}, u32[]{:S(2)}, u32[]{:S(2)}) collective-permute-start(bf16[512,128]{1,0:T(8,128)(2,1)S(1)} %get-tuple-element.32), channel_id=1, source_target_pairs={{0,8},{4,12},{8,0},{12,4},{16,24},{20,28},{24,16},{28,20},{1,9},{5... | collective-permute-start | bytes 393224 | tf_op jit(solution)/shard_map/ppermute | solution.py:305
  102.7 2.9 %collective-permute-done.16.refs_1_ = bf16[512,128]{1,0:T(8,128)(2,1)S(1)} collective-permute-done((bf16[512,128]{1,0:T(8,128)(2,1)S(1)}, bf16[512,128]{1,0:T(8,128)(2,1)S(1)}, u32[]{:S(2)}, u32[]{:S(2)}) %collective-permute-start.16) | collective-permute-done | bytes 131104 | tf_op jit(solution)/shard_map/ppermute | solution.py:305
  106.8 3.5 %shard_map.109 = (bf16[256,1024]{1,0:T(8,128)(2,1)}, f32[256,1024]{1,0:T(8,128)S(1)}, f32[256,1024]{1,0:T(8,128)S(1)}) custom-call(bf16[256,1024]{1,0:T(8,128)(2,1)S(1)} %copy-done.5, bf16[256,1024]{1,0:T(8,128)(2,1)S(1)} %copy-done.1, bf16[256,1024]{1,0:T(8,128)(2,1)S(1)} %copy-done.3, bf16[256,1024]{1,0:T(8,128)(2,1)S(1)} %get-tuple-element.26.d, ...), custom_call_target="tpu_custom_call" | custom-call | tf_op jit(solution)/shard_map/pallas_call | solution.py:44
  111.0 1.7 %shard_map.113 = (bf16[256,1024]{1,0:T(8,128)(2,1)}, bf16[256,1024]{1,0:T(8,128)(2,1)}) custom-call(bf16[256,1024]{1,0:T(8,128)(2,1)S(1)} %copy-done.1, bf16[256,1024]{1,0:T(8,128)(2,1)S(1)} %copy-done.3, f32[256,1024]{1,0:T(8,128)S(1)} %get-tuple-element.28.part_k, f32[256,1024]{1,0:T(8,128)S(1)} %get-tuple-element.29.part_v, f32[1024,128]{1,0:T(8,128)S(1)} %shard_map.112.suffix), custom_call_target="tpu_custom_call" | custom-call | tf_op jit(solution)/shard_map/pallas_call | solution.py:44
  113.0 2.1 %shard_map.104 = bf16[256,1024]{1,0:T(8,128)(2,1)} custom-call(s32[2]{0:T(128)S(1)} %compare_select_fusion.at, bf16[1024,4096]{1,0:T(8,128)(2,1)S(1)} %bitcast.1, bf16[256,1024]{1,0:T(8,128)(2,1)S(1)} %get-tuple-element.24.normed.refs_0_, bf16[256,1024]{1,0:T(8,128)(2,1)S(1)} %collective-permute-done.9.refs_0_, ...), custom_call_target="tpu_custom_call" | custom-call | tf_op jit(solution)/shard_map/pallas_call | solution.py:44
  115.1 2.3 %shard_map.118 = f32[1024,512]{1,0:T(8,128)} custom-call(s32[2]{0:T(128)S(1)} %compare_select_fusion.at, f32[1024,1024]{1,0:T(8,128)S(1)} %shard_map.115.so_far, bf16[256,1024]{1,0:T(8,128)(2,1)S(1)} %collective-permute-done.23.rows, bf16[256,1024]{1,0:T(8,128)(2,1)S(1)} %collective-permute-done.24.cols, bf16[1024,512]{1,0:T(8,128)(2,1)S(1)} %collective-permute-done.25.refs_0_), custom_call_target="tpu_custom_call" | custom-call | tf_op jit(solution)/shard_map/pallas_call | solution.py:44
  (67 shorter events, 23.6 us)
Async XLA Ops:
  0.6 31.7 %copy-start.5 = (bf16[256,1024]{1,0:T(8,128)(2,1)S(1)}, bf16[256,1024]{1,0:T(8,128)(2,1)}, u32[]{:S(2)}) copy-start(bf16[256,1024]{1,0:T(8,128)(2,1)} %q.7) | copy-start | bytes 1572868
  0.6 15.3 %collective-permute-start.5 = (bf16[256,1024]{1,0:T(8,128)(2,1)}, bf16[256,1024]{1,0:T(8,128)(2,1)S(1)}, u32[]{:S(2)}, u32[]{:S(2)}) collective-permute-start(bf16[256,1024]{1,0:T(8,128)(2,1)} %refs_0_.1), channel_id=1, source_target_pairs={{0,1},{1,0},{2,3},{3,2},{4,5},{5,4},{6,7},{7,6},{8,9},{9,8},{10,11... | collective-permute-start | bytes 1572872 | tf_op jit(solution)/shard_map/ppermute | solution.py:346
  5.5 11.1 %collective-permute-start = (f32[1024,128]{1,0:T(8,128)S(1)}, f32[1024,128]{1,0:T(8,128)S(1)}, u32[]{:S(2)}, u32[]{:S(2)}) collective-permute-start(f32[1024,128]{1,0:T(8,128)S(1)} %shard_map.93.block), channel_id=1, source_target_pairs={{0,4},{4,0},{8,12},{12,8},{16,20},{20,16},{24,28},{28,24},{1,5},{5... | collective-permute-start | bytes 1572872 | tf_op jit(solution)/shard_map/ppermute | solution.py:293
  5.5 24.9 %collective-permute-start.12 = (bf16[256,1024]{1,0:T(8,128)(2,1)}, bf16[256,1024]{1,0:T(8,128)(2,1)S(1)}, u32[]{:S(2)}, u32[]{:S(2)}) collective-permute-start(bf16[256,1024]{1,0:T(8,128)(2,1)} %refs_0_.1), channel_id=1, source_target_pairs={{1,2},{2,1},{5,6},{6,5},{9,10},{10,9},{13,14},{14,13},{17,18},{18,... | collective-permute-start | bytes 1572872 | tf_op jit(solution)/shard_map/ppermute | solution.py:346
  15.9 20.0 %collective-permute-start.6 = (bf16[256,1024]{1,0:T(8,128)(2,1)S(1)}, bf16[256,1024]{1,0:T(8,128)(2,1)S(1)}, u32[]{:S(2)}, u32[]{:S(2)}) collective-permute-start(bf16[256,1024]{1,0:T(8,128)(2,1)S(1)} %collective-permute-done.5.refs_0_.refs_1_), channel_id=1, source_target_pairs={{1,2},{2,1},{5,6},{6,5},{9,10},{10,9},{13,14},{14,13},{17,18},{18,... | collective-permute-start | bytes 1572872 | tf_op jit(solution)/shard_map/ppermute | solution.py:346
  17.2 6.7 %collective-permute-start.3 = (bf16[512,128]{1,0:T(8,128)(2,1)S(1)}, bf16[512,128]{1,0:T(8,128)(2,1)S(1)}, u32[]{:S(2)}, u32[]{:S(2)}) collective-permute-start(bf16[512,128]{1,0:T(8,128)(2,1)S(1)} %get-tuple-element.23), channel_id=1, source_target_pairs={{0,24},{4,28},{8,16},{12,20},{16,8},{20,12},{24,0},{28,4},{1,25},{... | collective-permute-start | bytes 393224 | tf_op jit(solution)/shard_map/ppermute | solution.py:305
  19.9 5.8 %collective-permute-start.2 = (bf16[512,128]{1,0:T(8,128)(2,1)S(1)}, bf16[512,128]{1,0:T(8,128)(2,1)S(1)}, u32[]{:S(2)}, u32[]{:S(2)}) collective-permute-start(bf16[512,128]{1,0:T(8,128)(2,1)S(1)} %get-tuple-element.23), channel_id=1, source_target_pairs={{0,16},{4,20},{8,24},{12,28},{16,0},{20,4},{24,8},{28,12},{1,17},{... | collective-permute-start | bytes 393224 | tf_op jit(solution)/shard_map/ppermute | solution.py:305
  20.4 5.3 %collective-permute-start.1 = (bf16[512,128]{1,0:T(8,128)(2,1)S(1)}, bf16[512,128]{1,0:T(8,128)(2,1)S(1)}, u32[]{:S(2)}, u32[]{:S(2)}) collective-permute-start(bf16[512,128]{1,0:T(8,128)(2,1)S(1)} %get-tuple-element.23), channel_id=1, source_target_pairs={{0,8},{4,12},{8,0},{12,4},{16,24},{20,28},{24,16},{28,20},{1,9},{5... | collective-permute-start | bytes 393224 | tf_op jit(solution)/shard_map/ppermute | solution.py:305
  26.3 5.5 %collective-permute-start.4 = (f32[512,128]{1,0:T(8,128)S(1)}, f32[512,128]{1,0:T(8,128)S(1)}, u32[]{:S(2)}, u32[]{:S(2)}) collective-permute-start(f32[512,128]{1,0:T(8,128)S(1)} %shard_map.95.mine), channel_id=1, source_target_pairs={{0,4},{4,0},{8,12},{12,8},{16,20},{20,16},{24,28},{28,24},{1,5},{5... | collective-permute-start | bytes 786440 | tf_op jit(solution)/shard_map/ppermute | solution.py:307
  30.4 18.1 %collective-permute-start.13 = (bf16[256,1024]{1,0:T(8,128)(2,1)S(1)}, bf16[256,1024]{1,0:T(8,128)(2,1)S(1)}, u32[]{:S(2)}, u32[]{:S(2)}) collective-permute-start(bf16[256,1024]{1,0:T(8,128)(2,1)S(1)} %collective-permute-done.12.refs_1_.refs_2_), channel_id=1, source_target_pairs={{1,0},{2,3},{5,4},{6,7},{9,8},{10,11},{13,12},{14,15},{17,16},{18,... | collective-permute-start | bytes 1572872 | tf_op jit(solution)/shard_map/ppermute | solution.py:346
  32.9 33.3 %slice-start = ((s8[8388608]{0:T(1024)(128)(4,1)}), s8[4194304]{0:T(1024)(128)(4,1)S(1)}, s32[]{:S(2)}) async-start(s8[8388608]{0:T(1024)(128)(4,1)} %bitcast), calls=%async_computation | async-start | bytes 8388608
  33.0 26.6 %copy-start.6 = (bf16[256,1024]{1,0:T(8,128)(2,1)S(1)}, bf16[256,1024]{1,0:T(8,128)(2,1)}, u32[]{:S(2)}) copy-start(bf16[256,1024]{1,0:T(8,128)(2,1)} %refs_0_.1) | copy-start | bytes 1572868
  33.0 33.3 %slice-start.1 = ((s8[8388608]{0:T(1024)(128)(4,1)}), s8[4194304]{0:T(1024)(128)(4,1)S(1)}, s32[]{:S(2)}) async-start(s8[8388608]{0:T(1024)(128)(4,1)} %bitcast), calls=%async_computation.1 | async-start | bytes 8388608
  36.5 23.1 %collective-permute-start.7 = (bf16[256,1024]{1,0:T(8,128)(2,1)S(1)}, bf16[256,1024]{1,0:T(8,128)(2,1)S(1)}, u32[]{:S(2)}, u32[]{:S(2)}) collective-permute-start(bf16[256,1024]{1,0:T(8,128)(2,1)S(1)} %shard_map.99), channel_id=1, source_target_pairs={{1,0},{2,3},{0,1},{3,2},{5,4},{6,7},{4,5},{7,6},{9,8},{10,11},{8,9... | collective-permute-start | bytes 1572872 | tf_op jit(solution)/shard_map/ppermute | solution.py:392
  40.6 22.2 %collective-permute-start.20 = (bf16[256,1024]{1,0:T(8,128)(2,1)S(1)}, bf16[256,1024]{1,0:T(8,128)(2,1)S(1)}, u32[]{:S(2)}, u32[]{:S(2)}) collective-permute-start(bf16[256,1024]{1,0:T(8,128)(2,1)S(1)} %get-tuple-element.24.normed.refs_0_), channel_id=1, source_target_pairs={{0,16},{4,20},{8,24},{12,28},{16,0},{20,4},{24,8},{28,12},{1,17},{... | collective-permute-start | bytes 1572872 | tf_op jit(solution)/shard_map/ppermute | solution.py:410
  42.2 20.7 %collective-permute-start.19 = (bf16[256,1024]{1,0:T(8,128)(2,1)S(1)}, bf16[256,1024]{1,0:T(8,128)(2,1)S(1)}, u32[]{:S(2)}, u32[]{:S(2)}) collective-permute-start(bf16[256,1024]{1,0:T(8,128)(2,1)S(1)} %get-tuple-element.24.normed.refs_0_), channel_id=1, source_target_pairs={{0,8},{4,12},{8,0},{12,4},{16,24},{20,28},{24,16},{28,20},{1,9},{5... | collective-permute-start | bytes 1572872 | tf_op jit(solution)/shard_map/ppermute | solution.py:410
  60.5 15.0 %collective-permute-start.21 = (bf16[256,1024]{1,0:T(8,128)(2,1)S(1)}, bf16[256,1024]{1,0:T(8,128)(2,1)S(1)}, u32[]{:S(2)}, u32[]{:S(2)}) collective-permute-start(bf16[256,1024]{1,0:T(8,128)(2,1)S(1)} %get-tuple-element.36), channel_id=1, source_target_pairs={{0,8},{4,12},{8,0},{12,4},{16,24},{20,28},{24,16},{28,20},{1,9},{5... | collective-permute-start | bytes 1572872 | tf_op jit(solution)/shard_map/ppermute | solution.py:466
  62.1 17.4 %collective-permute-start.22 = (bf16[256,1024]{1,0:T(8,128)(2,1)S(1)}, bf16[256,1024]{1,0:T(8,128)(2,1)S(1)}, u32[]{:S(2)}, u32[]{:S(2)}) collective-permute-start(bf16[256,1024]{1,0:T(8,128)(2,1)S(1)} %get-tuple-element.37), channel_id=1, source_target_pairs={{0,16},{4,20},{8,24},{12,28},{16,0},{20,4},{24,8},{28,12},{1,17},{... | collective-permute-start | bytes 1572872 | tf_op jit(solution)/shard_map/ppermute | solution.py:466
  63.4 22.1 %collective-permute-start.23 = (bf16[256,1024]{1,0:T(8,128)(2,1)S(1)}, bf16[256,1024]{1,0:T(8,128)(2,1)S(1)}, u32[]{:S(2)}, u32[]{:S(2)}) collective-permute-start(bf16[256,1024]{1,0:T(8,128)(2,1)S(1)} %shard_map.116), channel_id=1, source_target_pairs={{0,8},{4,20},{8,0},{12,28},{16,24},{20,4},{24,16},{28,12},{1,9},{5... | collective-permute-start | bytes 1572872 | tf_op jit(solution)/shard_map/ppermute | solution.py:410
  64.8 27.4 %collective-permute-start.24 = (bf16[256,1024]{1,0:T(8,128)(2,1)S(1)}, bf16[256,1024]{1,0:T(8,128)(2,1)S(1)}, u32[]{:S(2)}, u32[]{:S(2)}) collective-permute-start(bf16[256,1024]{1,0:T(8,128)(2,1)S(1)} %get-tuple-element.38), channel_id=1, source_target_pairs={{0,24},{4,28},{8,16},{12,20},{16,8},{20,12},{24,0},{28,4},{1,25},{... | collective-permute-start | bytes 1572872 | tf_op jit(solution)/shard_map/ppermute | solution.py:466
  72.9 20.5 %collective-permute-start.14 = (f32[1024,128]{1,0:T(8,128)S(1)}, f32[1024,128]{1,0:T(8,128)S(1)}, u32[]{:S(2)}, u32[]{:S(2)}) collective-permute-start(f32[1024,128]{1,0:T(8,128)S(1)} %get-tuple-element.30.block), channel_id=1, source_target_pairs={{0,4},{4,0},{8,12},{12,8},{16,20},{20,16},{24,28},{28,24},{1,5},{5... | collective-permute-start | bytes 1572872 | tf_op jit(solution)/shard_map/ppermute | solution.py:293
  75.5 20.0 %collective-permute-start.10 = (bf16[256,1024]{1,0:T(8,128)(2,1)S(1)}, bf16[256,1024]{1,0:T(8,128)(2,1)S(1)}, u32[]{:S(2)}, u32[]{:S(2)}) collective-permute-start(bf16[256,1024]{1,0:T(8,128)(2,1)S(1)} %shard_map.102), channel_id=1, source_target_pairs={{0,1},{3,2},{4,5},{7,6},{8,9},{11,10},{12,13},{15,14},{16,17},{19,... | collective-permute-start | bytes 1572872 | tf_op jit(solution)/shard_map/ppermute | solution.py:384
  79.5 18.2 %collective-permute-start.8 = (bf16[256,1024]{1,0:T(8,128)(2,1)S(1)}, bf16[256,1024]{1,0:T(8,128)(2,1)S(1)}, u32[]{:S(2)}, u32[]{:S(2)}) collective-permute-start(bf16[256,1024]{1,0:T(8,128)(2,1)S(1)} %shard_map.100), channel_id=1, source_target_pairs={{2,1},{1,2},{6,5},{5,6},{10,9},{9,10},{14,13},{13,14},{18,17},{17,... | collective-permute-start | bytes 1572872 | tf_op jit(solution)/shard_map/ppermute | solution.py:384
  93.2 21.8 %collective-permute-start.25 = (bf16[1024,512]{1,0:T(8,128)(2,1)S(1)}, bf16[1024,512]{1,0:T(8,128)(2,1)S(1)}, u32[]{:S(2)}, u32[]{:S(2)}) collective-permute-start(bf16[1024,512]{1,0:T(8,128)(2,1)S(1)} %shard_map.117), channel_id=1, source_target_pairs={{0,4},{4,0},{8,12},{12,8},{16,20},{20,16},{24,28},{28,24},{1,5},{5... | collective-permute-start | bytes 3145736 | tf_op jit(solution)/shard_map/ppermute | solution.py:493
  94.0 7.1 %collective-permute-start.17 = (bf16[512,128]{1,0:T(8,128)(2,1)S(1)}, bf16[512,128]{1,0:T(8,128)(2,1)S(1)}, u32[]{:S(2)}, u32[]{:S(2)}) collective-permute-start(bf16[512,128]{1,0:T(8,128)(2,1)S(1)} %get-tuple-element.32), channel_id=1, source_target_pairs={{0,24},{4,28},{8,16},{12,20},{16,8},{20,12},{24,0},{28,4},{1,25},{... | collective-permute-start | bytes 393224 | tf_op jit(solution)/shard_map/ppermute | solution.py:305
  96.8 10.0 %copy-start.1 = (bf16[256,1024]{1,0:T(8,128)(2,1)S(1)}, bf16[256,1024]{1,0:T(8,128)(2,1)}, u32[]{:S(2)}) copy-start(bf16[256,1024]{1,0:T(8,128)(2,1)} %k.5) | copy-start | bytes 1572868
  96.8 10.0 %copy-start.3 = (bf16[256,1024]{1,0:T(8,128)(2,1)S(1)}, bf16[256,1024]{1,0:T(8,128)(2,1)}, u32[]{:S(2)}) copy-start(bf16[256,1024]{1,0:T(8,128)(2,1)} %v.5) | copy-start | bytes 1572868
  96.8 15.8 %collective-permute-start.11 = (bf16[256,1024]{1,0:T(8,128)(2,1)S(1)}, bf16[256,1024]{1,0:T(8,128)(2,1)S(1)}, u32[]{:S(2)}, u32[]{:S(2)}) collective-permute-start(bf16[256,1024]{1,0:T(8,128)(2,1)S(1)} %shard_map.103), channel_id=1, source_target_pairs={{2,1},{1,2},{6,5},{5,6},{10,9},{9,10},{14,13},{13,14},{18,17},{17,... | collective-permute-start | bytes 1572872 | tf_op jit(solution)/shard_map/ppermute | solution.py:384
  99.0 14.0 %collective-permute-start.9 = (bf16[256,1024]{1,0:T(8,128)(2,1)S(1)}, bf16[256,1024]{1,0:T(8,128)(2,1)S(1)}, u32[]{:S(2)}, u32[]{:S(2)}) collective-permute-start(bf16[256,1024]{1,0:T(8,128)(2,1)S(1)} %shard_map.101), channel_id=1, source_target_pairs={{1,0},{0,1},{3,2},{2,3},{5,4},{4,5},{7,6},{6,7},{9,8},{8,9},{11,10... | collective-permute-start | bytes 1572872 | tf_op jit(solution)/shard_map/ppermute | solution.py:384
  100.7 5.0 %collective-permute-start.16 = (bf16[512,128]{1,0:T(8,128)(2,1)S(1)}, bf16[512,128]{1,0:T(8,128)(2,1)S(1)}, u32[]{:S(2)}, u32[]{:S(2)}) collective-permute-start(bf16[512,128]{1,0:T(8,128)(2,1)S(1)} %get-tuple-element.32), channel_id=1, source_target_pairs={{0,16},{4,20},{8,24},{12,28},{16,0},{20,4},{24,8},{28,12},{1,17},{... | collective-permute-start | bytes 393224 | tf_op jit(solution)/shard_map/ppermute | solution.py:305
  101.1 5.0 %collective-permute-start.15 = (bf16[512,128]{1,0:T(8,128)(2,1)S(1)}, bf16[512,128]{1,0:T(8,128)(2,1)S(1)}, u32[]{:S(2)}, u32[]{:S(2)}) collective-permute-start(bf16[512,128]{1,0:T(8,128)(2,1)S(1)} %get-tuple-element.32), channel_id=1, source_target_pairs={{0,8},{4,12},{8,0},{12,4},{16,24},{20,28},{24,16},{28,20},{1,9},{5... | collective-permute-start | bytes 393224 | tf_op jit(solution)/shard_map/ppermute | solution.py:305
  106.7 3.6 %collective-permute-start.18 = (f32[512,128]{1,0:T(8,128)S(1)}, f32[512,128]{1,0:T(8,128)S(1)}, u32[]{:S(2)}, u32[]{:S(2)}) collective-permute-start(f32[512,128]{1,0:T(8,128)S(1)} %shard_map.111.mine), channel_id=1, source_target_pairs={{0,4},{4,0},{8,12},{12,8},{16,20},{20,16},{24,28},{28,24},{1,5},{5... | collective-permute-start | bytes 786440 | tf_op jit(solution)/shard_map/ppermute | solution.py:307
  (3 other events, 3.1 us)
where the time goes:
time: 118 us; the launch traced here: 117 us
  waiting for transfers between devices  47.5 us (40%)
  Pallas kernels  36 us (31%)
  starting transfers between devices  29.7 us (25%)
  local copies, waits for them, and re-layouts  3.16 us (3%)
    pallas_call x27, Pallas kernels, kernel_call(): pl.pallas_call(kernel, compiler_params=pltpu.CompilerParams(vmem_limit_by...  36 us
    ppermute x4, waiting for transfers between devices, body(): got[r, p] = lax.ppermute(got[r - 1, 1 - p], 'head', line(r, p))  15.3 us
    ppermute x1, waiting for transfers between devices, body(): got[r, p] = came[r, p] = lax.ppermute(sent, 'head', line(r, p) + back)  11 us
    ppermute x3, waiting for transfers between devices, body(): cols[n + 1] = lax.ppermute(cols[n + 1], 'ctx', flipped(n_ctx, mask))  9.19 us
    ppermute x6, waiting for transfers between devices, exclusive_sum(): others.append(lax.ppermute(sent, 'ctx', flipped(n_ctx, mask)))  8.27 us
    ppermute x6, starting transfers between devices, exclusive_sum(): others.append(lax.ppermute(sent, 'ctx', flipped(n_ctx, mask)))  7.14 us
    ppermute x4, starting transfers between devices, body(): got[r, p] = lax.ppermute(got[r - 1, 1 - p], 'head', line(r, p))  5.79 us
    ppermute x4, starting transfers between devices, body(): came[r, p] = lax.ppermute(sent, 'head', back)  4.86 us
  transfers between devices with their start and end apart: 26, of which 11 were waited for; matrix products, arithmetic and copies ran while one was open for 0% of the time, Pallas kernels for 29%

commit v1 on v0

--- a/solution.py
+++ b/solution.py
@@ -248,6 +248,24 @@
     for ref in extras:
         value = value + ref[...].astype(f32)
     out[...] = value.astype(out.dtype)
+
+
+def weight_out_kernel(core_of, at, so_far, rows, cols, *refs):
+    extras, (out, buffer, sems) = refs[:-3], refs[-3:]
+    chunks, size, own_cols = buffer.shape
+    core = core_of(at[1])
+    mine = pl.ds(pl.multiple_of(core * own_cols, own_cols), own_cols)
+    copies = []
+    for c in range(chunks):
+        cut = slice(c * size, (c + 1) * size)
+        value = so_far[cut, mine] + mm(rows[:, cut], cols[:, mine], 0, 0)
+        for ref in extras:
+            value = value + ref[cut, :].astype(f32)
+        buffer[c] = value
+        copies.append(pltpu.make_async_copy(buffer.at[c], out.at[pl.ds(c * size, size), :], sems.at[c]))
+        copies[-1].start()
+    for copy in copies:
+        copy.wait()
 
 
 def flipped(size, mask):
@@ -491,7 +509,22 @@
         if pair > 1:
             other = weight_last(partner, bf16)
             extra = [lax.ppermute(other, "ctx", flipped(n_ctx, 1))]
-        grad_out_weight = weight_last(same, f32, *extra)
+        pieces_out = 4 if width % (4 * HEAD_DIM) == 0 else 1
+        grad_out_weight = kernel_call(
+            functools.partial(weight_out_kernel, same),
+            where,
+            so_far,
+            rows[-1],
+            cols[-1],
+            *extra,
+            out_shape=array((width, own_cols), f32),
+            in_specs=[pl.BlockSpec(memory_space=pltpu.SMEM)] + [VMEM] * (3 + len(extra)),
+            out_specs=pl.BlockSpec(memory_space=pltpu.HBM),
+            scratch_shapes=[
+                pltpu.VMEM((pieces_out, width // pieces_out, own_cols), f32),
+                pltpu.SemaphoreType.DMA((pieces_out,)),
+            ],
+        )
         return mixed, grad_q, grad_k, grad_v, grad_out_weight
 
     return body

time: 118 us -> 118 us (level)
  no operation moved by 1% of the time
where the time goes in v1:
time: 118 us; the launch traced here: 117 us
  waiting for transfers between devices  47.5 us (40%)
  Pallas kernels  35.8 us (30%)
  starting transfers between devices  29.7 us (25%)
  local copies, waits for them, and re-layouts  3.16 us (3%)
  between operations  1.21 us (1%)
    pallas_call x27, Pallas kernels, kernel_call(): pl.pallas_call(kernel, compiler_params=pltpu.CompilerParams(vmem_limit_by...  35.8 us
    ppermute x4, waiting for transfers between devices, body(): got[r, p] = lax.ppermute(got[r - 1, 1 - p], 'head', line(r, p))  15.3 us
    ppermute x1, waiting for transfers between devices, body(): got[r, p] = came[r, p] = lax.ppermute(sent, 'head', line(r, p) + back)  11 us
    ppermute x3, waiting for transfers between devices, body(): cols[n + 1] = lax.ppermute(cols[n + 1], 'ctx', flipped(n_ctx, mask))  9.19 us
    ppermute x6, waiting for transfers between devices, exclusive_sum(): others.append(lax.ppermute(sent, 'ctx', flipped(n_ctx, mask)))  8.27 us
    ppermute x6, starting transfers between devices, exclusive_sum(): others.append(lax.ppermute(sent, 'ctx', flipped(n_ctx, mask)))  7.14 us
    ppermute x4, starting transfers between devices, body(): got[r, p] = lax.ppermute(got[r - 1, 1 - p], 'head', line(r, p))  5.79 us
    ppermute x4, starting transfers between devices, body(): came[r, p] = lax.ppermute(sent, 'head', back)  4.86 us
  transfers between devices with their start and end apart: 26, of which 11 were waited for; matrix products, arithmetic and copies ran while one was open for 0% of the time, Pallas kernels for 29%

profile of v1, /device:TPU:0, one launch (start us, length us, event | category | flops | bytes accessed | tf_op | source)
XLA Modules:
  0.0 117.4 jit_solution(16651419081832775545)
XLA Ops:
  0.6 3.1 %collective-permute-start.5 = (bf16[256,1024]{1,0:T(8,128)(2,1)}, bf16[256,1024]{1,0:T(8,128)(2,1)S(1)}, u32[]{:S(2)}, u32[]{:S(2)}) collective-permute-start(bf16[256,1024]{1,0:T(8,128)(2,1)} %refs_0_.1), channel_id=1, source_target_pairs={{0,1},{1,0},{2,3},{3,2},{4,5},{5,4},{6,7},{7,6},{8,9},{9,8},{10,11... | collective-permute-start | bytes 1572872 | tf_op jit(solution)/shard_map/ppermute | solution.py:364
  3.8 1.7 %shard_map.93.block = f32[1024,128]{1,0:T(8,128)S(1)} custom-call(bf16[256,1024]{1,0:T(8,128)(2,1)} %k.5, bf16[256,1024]{1,0:T(8,128)(2,1)} %v.5), custom_call_target="tpu_custom_call" | custom-call | tf_op jit(solution)/shard_map/pallas_call | solution.py:44
  6.3 9.6 %collective-permute-done.5.refs_0_.refs_1_ = bf16[256,1024]{1,0:T(8,128)(2,1)S(1)} collective-permute-done((bf16[256,1024]{1,0:T(8,128)(2,1)}, bf16[256,1024]{1,0:T(8,128)(2,1)S(1)}, u32[]{:S(2)}, u32[]{:S(2)}) %collective-permute-start.5) | collective-permute-done | bytes 524320 | tf_op jit(solution)/shard_map/ppermute | solution.py:364
  17.2 2.7 %collective-permute-start.3 = (bf16[512,128]{1,0:T(8,128)(2,1)S(1)}, bf16[512,128]{1,0:T(8,128)(2,1)S(1)}, u32[]{:S(2)}, u32[]{:S(2)}) collective-permute-start(bf16[512,128]{1,0:T(8,128)(2,1)S(1)} %get-tuple-element.23), channel_id=1, source_target_pairs={{0,24},{4,28},{8,16},{12,20},{16,8},{20,12},{24,0},{28,4},{1,25},{... | collective-permute-start | bytes 393224 | tf_op jit(solution)/shard_map/ppermute | solution.py:323
  20.8 3.1 %collective-permute-done.3.refs_2_ = bf16[512,128]{1,0:T(8,128)(2,1)S(1)} collective-permute-done((bf16[512,128]{1,0:T(8,128)(2,1)S(1)}, bf16[512,128]{1,0:T(8,128)(2,1)S(1)}, u32[]{:S(2)}, u32[]{:S(2)}) %collective-permute-start.3) | collective-permute-done | bytes 131104 | tf_op jit(solution)/shard_map/ppermute | solution.py:323
  23.9 1.8 %collective-permute-done.2.refs_1_ = bf16[512,128]{1,0:T(8,128)(2,1)S(1)} collective-permute-done((bf16[512,128]{1,0:T(8,128)(2,1)S(1)}, bf16[512,128]{1,0:T(8,128)(2,1)S(1)}, u32[]{:S(2)}, u32[]{:S(2)}) %collective-permute-start.2) | collective-permute-done | bytes 131104 | tf_op jit(solution)/shard_map/ppermute | solution.py:323
  30.4 1.3 %collective-permute-start.13 = (bf16[256,1024]{1,0:T(8,128)(2,1)S(1)}, bf16[256,1024]{1,0:T(8,128)(2,1)S(1)}, u32[]{:S(2)}, u32[]{:S(2)}) collective-permute-start(bf16[256,1024]{1,0:T(8,128)(2,1)S(1)} %collective-permute-done.12.refs_1_.refs_2_), channel_id=1, source_target_pairs={{1,0},{2,3},{5,4},{6,7},{9,8},{10,11},{13,12},{14,15},{17,16},{18,... | collective-permute-start | bytes 1572872 | tf_op jit(solution)/shard_map/ppermute | solution.py:364
  33.0 2.9 %shard_map.98.refs_1_ = bf16[256,1024]{1,0:T(8,128)(2,1)S(1)} custom-call(s32[2]{0:T(128)S(1)} %compare_select_fusion.at, bf16[1024,4096]{1,0:T(8,128)(2,1)} %weight.19, bf16[256,1024]{1,0:T(8,128)(2,1)S(1)} %get-tuple-element.24.normed.refs_0_), custom_call_target="tpu_custom_call" | custom-call | tf_op jit(solution)/shard_map/pallas_call | solution.py:44
  36.5 4.2 %collective-permute-start.7 = (bf16[256,1024]{1,0:T(8,128)(2,1)S(1)}, bf16[256,1024]{1,0:T(8,128)(2,1)S(1)}, u32[]{:S(2)}, u32[]{:S(2)}) collective-permute-start(bf16[256,1024]{1,0:T(8,128)(2,1)S(1)} %shard_map.99), channel_id=1, source_target_pairs={{1,0},{2,3},{0,1},{3,2},{5,4},{6,7},{4,5},{7,6},{9,8},{10,11},{8,9... | collective-permute-start | bytes 1572872 | tf_op jit(solution)/shard_map/ppermute | solution.py:410
  40.6 1.5 %collective-permute-start.20 = (bf16[256,1024]{1,0:T(8,128)(2,1)S(1)}, bf16[256,1024]{1,0:T(8,128)(2,1)S(1)}, u32[]{:S(2)}, u32[]{:S(2)}) collective-permute-start(bf16[256,1024]{1,0:T(8,128)(2,1)S(1)} %get-tuple-element.24.normed.refs_0_), channel_id=1, source_target_pairs={{0,16},{4,20},{8,24},{12,28},{16,0},{20,4},{24,8},{28,12},{1,17},{... | collective-permute-start | bytes 1572872 | tf_op jit(solution)/shard_map/ppermute | solution.py:428
  42.9 5.6 %collective-permute-done.13.refs_0_.refs_3_ = bf16[256,1024]{1,0:T(8,128)(2,1)S(1)} collective-permute-done((bf16[256,1024]{1,0:T(8,128)(2,1)S(1)}, bf16[256,1024]{1,0:T(8,128)(2,1)S(1)}, u32[]{:S(2)}, u32[]{:S(2)}) %collective-permute-start.13) | collective-permute-done | bytes 524320 | tf_op jit(solution)/shard_map/ppermute | solution.py:364
  48.6 11.0 %collective-permute-done.7.refs_0_.refs_5_ = bf16[256,1024]{1,0:T(8,128)(2,1)S(1)} collective-permute-done((bf16[256,1024]{1,0:T(8,128)(2,1)S(1)}, bf16[256,1024]{1,0:T(8,128)(2,1)S(1)}, u32[]{:S(2)}, u32[]{:S(2)}) %collective-permute-start.7) | collective-permute-done | bytes 524320 | tf_op jit(solution)/shard_map/ppermute | solution.py:410
  60.5 1.6 %collective-permute-start.21 = (bf16[256,1024]{1,0:T(8,128)(2,1)S(1)}, bf16[256,1024]{1,0:T(8,128)(2,1)S(1)}, u32[]{:S(2)}, u32[]{:S(2)}) collective-permute-start(bf16[256,1024]{1,0:T(8,128)(2,1)S(1)} %get-tuple-element.36), channel_id=1, source_target_pairs={{0,8},{4,12},{8,0},{12,4},{16,24},{20,28},{24,16},{28,20},{1,9},{5... | collective-permute-start | bytes 1572872 | tf_op jit(solution)/shard_map/ppermute | solution.py:484
  63.4 1.4 %collective-permute-start.23 = (bf16[256,1024]{1,0:T(8,128)(2,1)S(1)}, bf16[256,1024]{1,0:T(8,128)(2,1)S(1)}, u32[]{:S(2)}, u32[]{:S(2)}) collective-permute-start(bf16[256,1024]{1,0:T(8,128)(2,1)S(1)} %shard_map.116), channel_id=1, source_target_pairs={{0,8},{4,20},{8,0},{12,28},{16,24},{20,4},{24,16},{28,12},{1,9},{5... | collective-permute-start | bytes 1572872 | tf_op jit(solution)/shard_map/ppermute | solution.py:428
  64.8 1.4 %collective-permute-start.24 = (bf16[256,1024]{1,0:T(8,128)(2,1)S(1)}, bf16[256,1024]{1,0:T(8,128)(2,1)S(1)}, u32[]{:S(2)}, u32[]{:S(2)}) collective-permute-start(bf16[256,1024]{1,0:T(8,128)(2,1)S(1)} %get-tuple-element.38), channel_id=1, source_target_pairs={{0,24},{4,28},{8,16},{12,20},{16,8},{20,12},{24,0},{28,4},{1,25},{... | collective-permute-start | bytes 1572872 | tf_op jit(solution)/shard_map/ppermute | solution.py:484
  66.2 1.3 %shard_map.105.first = f32[256,1024]{1,0:T(8,128)S(1)} custom-call(s32[2]{0:T(128)S(1)} %compare_select_fusion.at, bf16[1024,4096]{1,0:T(8,128)(2,1)S(1)} %bitcast.1, bf16[256,1024]{1,0:T(8,128)(2,1)S(1)} %copy-done.6), custom_call_target="tpu_custom_call" | custom-call | tf_op jit(solution)/shard_map/pallas_call | solution.py:44
  67.5 1.4 %shard_map.106.first = f32[256,1024]{1,0:T(8,128)S(1)} custom-call(s32[2]{0:T(128)S(1)} %compare_select_fusion.at, bf16[1024,4096]{1,0:T(8,128)(2,1)S(1)} %bitcast.1, f32[256,1024]{1,0:T(8,128)S(1)} %shard_map.105.first, bf16[256,1024]{1,0:T(8,128)(2,1)S(1)} %collective-permute-done.5.refs_0_.refs_1_, ...), custom_call_target="tpu_custom_call" | custom-call | tf_op jit(solution)/shard_map/pallas_call | solution.py:44
  68.9 1.4 %shard_map.107.so_far = f32[256,1024]{1,0:T(8,128)S(1)} custom-call(s32[2]{0:T(128)S(1)} %compare_select_fusion.at, bf16[1024,4096]{1,0:T(8,128)(2,1)S(1)} %bitcast.1, f32[256,1024]{1,0:T(8,128)S(1)} %shard_map.106.first, bf16[256,1024]{1,0:T(8,128)(2,1)S(1)} %collective-permute-done.13.refs_0_.refs_3_, ...), custom_call_target="tpu_custom_call" | custom-call | tf_op jit(solution)/shard_map/pallas_call | solution.py:44
  70.3 2.6 %shard_map.108 = (bf16[256,1024]{1,0:T(8,128)(2,1)S(1)}, f32[1024,128]{1,0:T(8,128)S(1)}) custom-call(s32[2]{0:T(128)S(1)} %compare_select_fusion.at, bf16[1024,4096]{1,0:T(8,128)(2,1)S(1)} %bitcast.1, f32[256,1024]{1,0:T(8,128)S(1)} %shard_map.107.so_far, f32[256,1024]{1,0:T(8,128)S(1)} %get-tuple-element.25.attended, bf16[256,1024]{1,0:T(8,128)(2,1)S(1)} %copy-done.5, ...), custom_call_target="tpu_custom_call" | custom-call | tf_op jit(solution)/shard_map/pallas_call | solution.py:44
  75.5 1.5 %collective-permute-start.10 = (bf16[256,1024]{1,0:T(8,128)(2,1)S(1)}, bf16[256,1024]{1,0:T(8,128)(2,1)S(1)}, u32[]{:S(2)}, u32[]{:S(2)}) collective-permute-start(bf16[256,1024]{1,0:T(8,128)(2,1)S(1)} %shard_map.102), channel_id=1, source_target_pairs={{0,1},{3,2},{4,5},{7,6},{8,9},{11,10},{12,13},{15,14},{16,17},{19,... | collective-permute-start | bytes 1572872 | tf_op jit(solution)/shard_map/ppermute | solution.py:402
  77.0 2.5 %collective-permute-done.22.refs_5_ = bf16[256,1024]{1,0:T(8,128)(2,1)S(1)} collective-permute-done((bf16[256,1024]{1,0:T(8,128)(2,1)S(1)}, bf16[256,1024]{1,0:T(8,128)(2,1)S(1)}, u32[]{:S(2)}, u32[]{:S(2)}) %collective-permute-start.22) | collective-permute-done | bytes 524320 | tf_op jit(solution)/shard_map/ppermute | solution.py:484
  80.4 1.8 %shard_map.115.so_far = f32[1024,1024]{1,0:T(8,128)S(1)} custom-call(bf16[256,1024]{1,0:T(8,128)(2,1)S(1)} %get-tuple-element.24.normed.refs_0_, bf16[256,1024]{1,0:T(8,128)(2,1)S(1)} %collective-permute-done.19.refs_1_, bf16[256,1024]{1,0:T(8,128)(2,1)S(1)} %collective-permute-done.20.refs_2_.refs_0_, bf16[256,1024]{1,0:T(8,128)(2,1)S(1)} %get-tuple-element.35.refs_3_, ...), custom_call_target="tpu_custom_call" | custom-call | tf_op jit(solution)/shard_map/pallas_call | solution.py:44
  82.2 3.3 %collective-permute-done.23.rows = bf16[256,1024]{1,0:T(8,128)(2,1)S(1)} collective-permute-done((bf16[256,1024]{1,0:T(8,128)(2,1)S(1)}, bf16[256,1024]{1,0:T(8,128)(2,1)S(1)}, u32[]{:S(2)}, u32[]{:S(2)}) %collective-permute-start.23) | collective-permute-done | bytes 524320 | tf_op jit(solution)/shard_map/ppermute | solution.py:428
  85.5 6.7 %collective-permute-done.24.cols = bf16[256,1024]{1,0:T(8,128)(2,1)S(1)} collective-permute-done((bf16[256,1024]{1,0:T(8,128)(2,1)S(1)}, bf16[256,1024]{1,0:T(8,128)(2,1)S(1)}, u32[]{:S(2)}, u32[]{:S(2)}) %collective-permute-start.24) | collective-permute-done | bytes 524320 | tf_op jit(solution)/shard_map/ppermute | solution.py:484
  94.0 1.5 %collective-permute-start.17 = (bf16[512,128]{1,0:T(8,128)(2,1)S(1)}, bf16[512,128]{1,0:T(8,128)(2,1)S(1)}, u32[]{:S(2)}, u32[]{:S(2)}) collective-permute-start(bf16[512,128]{1,0:T(8,128)(2,1)S(1)} %get-tuple-element.32), channel_id=1, source_target_pairs={{0,24},{4,28},{8,16},{12,20},{16,8},{20,12},{24,0},{28,4},{1,25},{... | collective-permute-start | bytes 393224 | tf_op jit(solution)/shard_map/ppermute | solution.py:323
  99.0 1.7 %collective-permute-start.9 = (bf16[256,1024]{1,0:T(8,128)(2,1)S(1)}, bf16[256,1024]{1,0:T(8,128)(2,1)S(1)}, u32[]{:S(2)}, u32[]{:S(2)}) collective-permute-start(bf16[256,1024]{1,0:T(8,128)(2,1)S(1)} %shard_map.101), channel_id=1, source_target_pairs={{1,0},{0,1},{3,2},{2,3},{5,4},{4,5},{7,6},{6,7},{9,8},{8,9},{11,10... | collective-permute-start | bytes 1572872 | tf_op jit(solution)/shard_map/ppermute | solution.py:402
  101.1 1.6 %collective-permute-start.15 = (bf16[512,128]{1,0:T(8,128)(2,1)S(1)}, bf16[512,128]{1,0:T(8,128)(2,1)S(1)}, u32[]{:S(2)}, u32[]{:S(2)}) collective-permute-start(bf16[512,128]{1,0:T(8,128)(2,1)S(1)} %get-tuple-element.32), channel_id=1, source_target_pairs={{0,8},{4,12},{8,0},{12,4},{16,24},{20,28},{24,16},{28,20},{1,9},{5... | collective-permute-start | bytes 393224 | tf_op jit(solution)/shard_map/ppermute | solution.py:323
  102.7 2.9 %collective-permute-done.16.refs_1_ = bf16[512,128]{1,0:T(8,128)(2,1)S(1)} collective-permute-done((bf16[512,128]{1,0:T(8,128)(2,1)S(1)}, bf16[512,128]{1,0:T(8,128)(2,1)S(1)}, u32[]{:S(2)}, u32[]{:S(2)}) %collective-permute-start.16) | collective-permute-done | bytes 131104 | tf_op jit(solution)/shard_map/ppermute | solution.py:323
  106.8 3.5 %shard_map.109 = (bf16[256,1024]{1,0:T(8,128)(2,1)}, f32[256,1024]{1,0:T(8,128)S(1)}, f32[256,1024]{1,0:T(8,128)S(1)}) custom-call(bf16[256,1024]{1,0:T(8,128)(2,1)S(1)} %copy-done.5, bf16[256,1024]{1,0:T(8,128)(2,1)S(1)} %copy-done.1, bf16[256,1024]{1,0:T(8,128)(2,1)S(1)} %copy-done.3, bf16[256,1024]{1,0:T(8,128)(2,1)S(1)} %get-tuple-element.26.d, ...), custom_call_target="tpu_custom_call" | custom-call | tf_op jit(solution)/shard_map/pallas_call | solution.py:44
  111.0 1.7 %shard_map.113 = (bf16[256,1024]{1,0:T(8,128)(2,1)}, bf16[256,1024]{1,0:T(8,128)(2,1)}) custom-call(bf16[256,1024]{1,0:T(8,128)(2,1)S(1)} %copy-done.1, bf16[256,1024]{1,0:T(8,128)(2,1)S(1)} %copy-done.3, f32[256,1024]{1,0:T(8,128)S(1)} %get-tuple-element.28.part_k, f32[256,1024]{1,0:T(8,128)S(1)} %get-tuple-element.29.part_v, f32[1024,128]{1,0:T(8,128)S(1)} %shard_map.112.suffix), custom_call_target="tpu_custom_call" | custom-call | tf_op jit(solution)/shard_map/pallas_call | solution.py:44
  113.0 2.1 %shard_map.104 = bf16[256,1024]{1,0:T(8,128)(2,1)} custom-call(s32[2]{0:T(128)S(1)} %compare_select_fusion.at, bf16[1024,4096]{1,0:T(8,128)(2,1)S(1)} %bitcast.1, bf16[256,1024]{1,0:T(8,128)(2,1)S(1)} %get-tuple-element.24.normed.refs_0_, bf16[256,1024]{1,0:T(8,128)(2,1)S(1)} %collective-permute-done.9.refs_0_, ...), custom_call_target="tpu_custom_call" | custom-call | tf_op jit(solution)/shard_map/pallas_call | solution.py:44
  115.1 2.2 %shard_map.118 = f32[1024,512]{1,0:T(8,128)} custom-call(s32[2]{0:T(128)S(1)} %compare_select_fusion.at, f32[1024,1024]{1,0:T(8,128)S(1)} %shard_map.115.so_far, bf16[256,1024]{1,0:T(8,128)(2,1)S(1)} %collective-permute-done.23.rows, bf16[256,1024]{1,0:T(8,128)(2,1)S(1)} %collective-permute-done.24.cols, bf16[1024,512]{1,0:T(8,128)(2,1)S(1)} %collective-permute-done.25.refs_0_), custom_call_target="tpu_custom_call" | custom-call | tf_op jit(solution)/shard_map/pallas_call | solution.py:44
  (67 shorter events, 23.6 us)
Async XLA Ops:
  0.6 31.7 %copy-start.5 = (bf16[256,1024]{1,0:T(8,128)(2,1)S(1)}, bf16[256,1024]{1,0:T(8,128)(2,1)}, u32[]{:S(2)}) copy-start(bf16[256,1024]{1,0:T(8,128)(2,1)} %q.7) | copy-start | bytes 1572868
  0.6 15.3 %collective-permute-start.5 = (bf16[256,1024]{1,0:T(8,128)(2,1)}, bf16[256,1024]{1,0:T(8,128)(2,1)S(1)}, u32[]{:S(2)}, u32[]{:S(2)}) collective-permute-start(bf16[256,1024]{1,0:T(8,128)(2,1)} %refs_0_.1), channel_id=1, source_target_pairs={{0,1},{1,0},{2,3},{3,2},{4,5},{5,4},{6,7},{7,6},{8,9},{9,8},{10,11... | collective-permute-start | bytes 1572872 | tf_op jit(solution)/shard_map/ppermute | solution.py:364
  5.5 11.1 %collective-permute-start = (f32[1024,128]{1,0:T(8,128)S(1)}, f32[1024,128]{1,0:T(8,128)S(1)}, u32[]{:S(2)}, u32[]{:S(2)}) collective-permute-start(f32[1024,128]{1,0:T(8,128)S(1)} %shard_map.93.block), channel_id=1, source_target_pairs={{0,4},{4,0},{8,12},{12,8},{16,20},{20,16},{24,28},{28,24},{1,5},{5... | collective-permute-start | bytes 1572872 | tf_op jit(solution)/shard_map/ppermute | solution.py:311
  5.5 24.9 %collective-permute-start.12 = (bf16[256,1024]{1,0:T(8,128)(2,1)}, bf16[256,1024]{1,0:T(8,128)(2,1)S(1)}, u32[]{:S(2)}, u32[]{:S(2)}) collective-permute-start(bf16[256,1024]{1,0:T(8,128)(2,1)} %refs_0_.1), channel_id=1, source_target_pairs={{1,2},{2,1},{5,6},{6,5},{9,10},{10,9},{13,14},{14,13},{17,18},{18,... | collective-permute-start | bytes 1572872 | tf_op jit(solution)/shard_map/ppermute | solution.py:364
  15.9 20.0 %collective-permute-start.6 = (bf16[256,1024]{1,0:T(8,128)(2,1)S(1)}, bf16[256,1024]{1,0:T(8,128)(2,1)S(1)}, u32[]{:S(2)}, u32[]{:S(2)}) collective-permute-start(bf16[256,1024]{1,0:T(8,128)(2,1)S(1)} %collective-permute-done.5.refs_0_.refs_1_), channel_id=1, source_target_pairs={{1,2},{2,1},{5,6},{6,5},{9,10},{10,9},{13,14},{14,13},{17,18},{18,... | collective-permute-start | bytes 1572872 | tf_op jit(solution)/shard_map/ppermute | solution.py:364
  17.2 6.7 %collective-permute-start.3 = (bf16[512,128]{1,0:T(8,128)(2,1)S(1)}, bf16[512,128]{1,0:T(8,128)(2,1)S(1)}, u32[]{:S(2)}, u32[]{:S(2)}) collective-permute-start(bf16[512,128]{1,0:T(8,128)(2,1)S(1)} %get-tuple-element.23), channel_id=1, source_target_pairs={{0,24},{4,28},{8,16},{12,20},{16,8},{20,12},{24,0},{28,4},{1,25},{... | collective-permute-start | bytes 393224 | tf_op jit(solution)/shard_map/ppermute | solution.py:323
  19.9 5.8 %collective-permute-start.2 = (bf16[512,128]{1,0:T(8,128)(2,1)S(1)}, bf16[512,128]{1,0:T(8,128)(2,1)S(1)}, u32[]{:S(2)}, u32[]{:S(2)}) collective-permute-start(bf16[512,128]{1,0:T(8,128)(2,1)S(1)} %get-tuple-element.23), channel_id=1, source_target_pairs={{0,16},{4,20},{8,24},{12,28},{16,0},{20,4},{24,8},{28,12},{1,17},{... | collective-permute-start | bytes 393224 | tf_op jit(solution)/shard_map/ppermute | solution.py:323
  20.4 5.3 %collective-permute-start.1 = (bf16[512,128]{1,0:T(8,128)(2,1)S(1)}, bf16[512,128]{1,0:T(8,128)(2,1)S(1)}, u32[]{:S(2)}, u32[]{:S(2)}) collective-permute-start(bf16[512,128]{1,0:T(8,128)(2,1)S(1)} %get-tuple-element.23), channel_id=1, source_target_pairs={{0,8},{4,12},{8,0},{12,4},{16,24},{20,28},{24,16},{28,20},{1,9},{5... | collective-permute-start | bytes 393224 | tf_op jit(solution)/shard_map/ppermute | solution.py:323
  26.3 5.5 %collective-permute-start.4 = (f32[512,128]{1,0:T(8,128)S(1)}, f32[512,128]{1,0:T(8,128)S(1)}, u32[]{:S(2)}, u32[]{:S(2)}) collective-permute-start(f32[512,128]{1,0:T(8,128)S(1)} %shard_map.95.mine), channel_id=1, source_target_pairs={{0,4},{4,0},{8,12},{12,8},{16,20},{20,16},{24,28},{28,24},{1,5},{5... | collective-permute-start | bytes 786440 | tf_op jit(solution)/shard_map/ppermute | solution.py:325
  30.4 18.1 %collective-permute-start.13 = (bf16[256,1024]{1,0:T(8,128)(2,1)S(1)}, bf16[256,1024]{1,0:T(8,128)(2,1)S(1)}, u32[]{:S(2)}, u32[]{:S(2)}) collective-permute-start(bf16[256,1024]{1,0:T(8,128)(2,1)S(1)} %collective-permute-done.12.refs_1_.refs_2_), channel_id=1, source_target_pairs={{1,0},{2,3},{5,4},{6,7},{9,8},{10,11},{13,12},{14,15},{17,16},{18,... | collective-permute-start | bytes 1572872 | tf_op jit(solution)/shard_map/ppermute | solution.py:364
  32.9 33.3 %slice-start = ((s8[8388608]{0:T(1024)(128)(4,1)}), s8[4194304]{0:T(1024)(128)(4,1)S(1)}, s32[]{:S(2)}) async-start(s8[8388608]{0:T(1024)(128)(4,1)} %bitcast), calls=%async_computation | async-start | bytes 8388608
  33.0 26.6 %copy-start.6 = (bf16[256,1024]{1,0:T(8,128)(2,1)S(1)}, bf16[256,1024]{1,0:T(8,128)(2,1)}, u32[]{:S(2)}) copy-start(bf16[256,1024]{1,0:T(8,128)(2,1)} %refs_0_.1) | copy-start | bytes 1572868
  33.0 33.3 %slice-start.1 = ((s8[8388608]{0:T(1024)(128)(4,1)}), s8[4194304]{0:T(1024)(128)(4,1)S(1)}, s32[]{:S(2)}) async-start(s8[8388608]{0:T(1024)(128)(4,1)} %bitcast), calls=%async_computation.1 | async-start | bytes 8388608
  36.5 23.1 %collective-permute-start.7 = (bf16[256,1024]{1,0:T(8,128)(2,1)S(1)}, bf16[256,1024]{1,0:T(8,128)(2,1)S(1)}, u32[]{:S(2)}, u32[]{:S(2)}) collective-permute-start(bf16[256,1024]{1,0:T(8,128)(2,1)S(1)} %shard_map.99), channel_id=1, source_target_pairs={{1,0},{2,3},{0,1},{3,2},{5,4},{6,7},{4,5},{7,6},{9,8},{10,11},{8,9... | collective-permute-start | bytes 1572872 | tf_op jit(solution)/shard_map/ppermute | solution.py:410
  40.6 22.2 %collective-permute-start.20 = (bf16[256,1024]{1,0:T(8,128)(2,1)S(1)}, bf16[256,1024]{1,0:T(8,128)(2,1)S(1)}, u32[]{:S(2)}, u32[]{:S(2)}) collective-permute-start(bf16[256,1024]{1,0:T(8,128)(2,1)S(1)} %get-tuple-element.24.normed.refs_0_), channel_id=1, source_target_pairs={{0,16},{4,20},{8,24},{12,28},{16,0},{20,4},{24,8},{28,12},{1,17},{... | collective-permute-start | bytes 1572872 | tf_op jit(solution)/shard_map/ppermute | solution.py:428
  42.2 20.7 %collective-permute-start.19 = (bf16[256,1024]{1,0:T(8,128)(2,1)S(1)}, bf16[256,1024]{1,0:T(8,128)(2,1)S(1)}, u32[]{:S(2)}, u32[]{:S(2)}) collective-permute-start(bf16[256,1024]{1,0:T(8,128)(2,1)S(1)} %get-tuple-element.24.normed.refs_0_), channel_id=1, source_target_pairs={{0,8},{4,12},{8,0},{12,4},{16,24},{20,28},{24,16},{28,20},{1,9},{5... | collective-permute-start | bytes 1572872 | tf_op jit(solution)/shard_map/ppermute | solution.py:428
  60.5 15.0 %collective-permute-start.21 = (bf16[256,1024]{1,0:T(8,128)(2,1)S(1)}, bf16[256,1024]{1,0:T(8,128)(2,1)S(1)}, u32[]{:S(2)}, u32[]{:S(2)}) collective-permute-start(bf16[256,1024]{1,0:T(8,128)(2,1)S(1)} %get-tuple-element.36), channel_id=1, source_target_pairs={{0,8},{4,12},{8,0},{12,4},{16,24},{20,28},{24,16},{28,20},{1,9},{5... | collective-permute-start | bytes 1572872 | tf_op jit(solution)/shard_map/ppermute | solution.py:484
  62.1 17.4 %collective-permute-start.22 = (bf16[256,1024]{1,0:T(8,128)(2,1)S(1)}, bf16[256,1024]{1,0:T(8,128)(2,1)S(1)}, u32[]{:S(2)}, u32[]{:S(2)}) collective-permute-start(bf16[256,1024]{1,0:T(8,128)(2,1)S(1)} %get-tuple-element.37), channel_id=1, source_target_pairs={{0,16},{4,20},{8,24},{12,28},{16,0},{20,4},{24,8},{28,12},{1,17},{... | collective-permute-start | bytes 1572872 | tf_op jit(solution)/shard_map/ppermute | solution.py:484
  63.4 22.1 %collective-permute-start.23 = (bf16[256,1024]{1,0:T(8,128)(2,1)S(1)}, bf16[256,1024]{1,0:T(8,128)(2,1)S(1)}, u32[]{:S(2)}, u32[]{:S(2)}) collective-permute-start(bf16[256,1024]{1,0:T(8,128)(2,1)S(1)} %shard_map.116), channel_id=1, source_target_pairs={{0,8},{4,20},{8,0},{12,28},{16,24},{20,4},{24,16},{28,12},{1,9},{5... | collective-permute-start | bytes 1572872 | tf_op jit(solution)/shard_map/ppermute | solution.py:428
  64.8 27.4 %collective-permute-start.24 = (bf16[256,1024]{1,0:T(8,128)(2,1)S(1)}, bf16[256,1024]{1,0:T(8,128)(2,1)S(1)}, u32[]{:S(2)}, u32[]{:S(2)}) collective-permute-start(bf16[256,1024]{1,0:T(8,128)(2,1)S(1)} %get-tuple-element.38), channel_id=1, source_target_pairs={{0,24},{4,28},{8,16},{12,20},{16,8},{20,12},{24,0},{28,4},{1,25},{... | collective-permute-start | bytes 1572872 | tf_op jit(solution)/shard_map/ppermute | solution.py:484
  72.9 20.5 %collective-permute-start.14 = (f32[1024,128]{1,0:T(8,128)S(1)}, f32[1024,128]{1,0:T(8,128)S(1)}, u32[]{:S(2)}, u32[]{:S(2)}) collective-permute-start(f32[1024,128]{1,0:T(8,128)S(1)} %get-tuple-element.30.block), channel_id=1, source_target_pairs={{0,4},{4,0},{8,12},{12,8},{16,20},{20,16},{24,28},{28,24},{1,5},{5... | collective-permute-start | bytes 1572872 | tf_op jit(solution)/shard_map/ppermute | solution.py:311
  75.5 20.0 %collective-permute-start.10 = (bf16[256,1024]{1,0:T(8,128)(2,1)S(1)}, bf16[256,1024]{1,0:T(8,128)(2,1)S(1)}, u32[]{:S(2)}, u32[]{:S(2)}) collective-permute-start(bf16[256,1024]{1,0:T(8,128)(2,1)S(1)} %shard_map.102), channel_id=1, source_target_pairs={{0,1},{3,2},{4,5},{7,6},{8,9},{11,10},{12,13},{15,14},{16,17},{19,... | collective-permute-start | bytes 1572872 | tf_op jit(solution)/shard_map/ppermute | solution.py:402
  79.5 18.2 %collective-permute-start.8 = (bf16[256,1024]{1,0:T(8,128)(2,1)S(1)}, bf16[256,1024]{1,0:T(8,128)(2,1)S(1)}, u32[]{:S(2)}, u32[]{:S(2)}) collective-permute-start(bf16[256,1024]{1,0:T(8,128)(2,1)S(1)} %shard_map.100), channel_id=1, source_target_pairs={{2,1},{1,2},{6,5},{5,6},{10,9},{9,10},{14,13},{13,14},{18,17},{17,... | collective-permute-start | bytes 1572872 | tf_op jit(solution)/shard_map/ppermute | solution.py:402
  93.2 21.8 %collective-permute-start.25 = (bf16[1024,512]{1,0:T(8,128)(2,1)S(1)}, bf16[1024,512]{1,0:T(8,128)(2,1)S(1)}, u32[]{:S(2)}, u32[]{:S(2)}) collective-permute-start(bf16[1024,512]{1,0:T(8,128)(2,1)S(1)} %shard_map.117), channel_id=1, source_target_pairs={{0,4},{4,0},{8,12},{12,8},{16,20},{20,16},{24,28},{28,24},{1,5},{5... | collective-permute-start | bytes 3145736 | tf_op jit(solution)/shard_map/ppermute | solution.py:511
  94.0 7.1 %collective-permute-start.17 = (bf16[512,128]{1,0:T(8,128)(2,1)S(1)}, bf16[512,128]{1,0:T(8,128)(2,1)S(1)}, u32[]{:S(2)}, u32[]{:S(2)}) collective-permute-start(bf16[512,128]{1,0:T(8,128)(2,1)S(1)} %get-tuple-element.32), channel_id=1, source_target_pairs={{0,24},{4,28},{8,16},{12,20},{16,8},{20,12},{24,0},{28,4},{1,25},{... | collective-permute-start | bytes 393224 | tf_op jit(solution)/shard_map/ppermute | solution.py:323
  96.8 10.0 %copy-start.1 = (bf16[256,1024]{1,0:T(8,128)(2,1)S(1)}, bf16[256,1024]{1,0:T(8,128)(2,1)}, u32[]{:S(2)}) copy-start(bf16[256,1024]{1,0:T(8,128)(2,1)} %k.5) | copy-start | bytes 1572868
  96.8 10.0 %copy-start.3 = (bf16[256,1024]{1,0:T(8,128)(2,1)S(1)}, bf16[256,1024]{1,0:T(8,128)(2,1)}, u32[]{:S(2)}) copy-start(bf16[256,1024]{1,0:T(8,128)(2,1)} %v.5) | copy-start | bytes 1572868
  96.8 15.8 %collective-permute-start.11 = (bf16[256,1024]{1,0:T(8,128)(2,1)S(1)}, bf16[256,1024]{1,0:T(8,128)(2,1)S(1)}, u32[]{:S(2)}, u32[]{:S(2)}) collective-permute-start(bf16[256,1024]{1,0:T(8,128)(2,1)S(1)} %shard_map.103), channel_id=1, source_target_pairs={{2,1},{1,2},{6,5},{5,6},{10,9},{9,10},{14,13},{13,14},{18,17},{17,... | collective-permute-start | bytes 1572872 | tf_op jit(solution)/shard_map/ppermute | solution.py:402
  99.0 14.0 %collective-permute-start.9 = (bf16[256,1024]{1,0:T(8,128)(2,1)S(1)}, bf16[256,1024]{1,0:T(8,128)(2,1)S(1)}, u32[]{:S(2)}, u32[]{:S(2)}) collective-permute-start(bf16[256,1024]{1,0:T(8,128)(2,1)S(1)} %shard_map.101), channel_id=1, source_target_pairs={{1,0},{0,1},{3,2},{2,3},{5,4},{4,5},{7,6},{6,7},{9,8},{8,9},{11,10... | collective-permute-start | bytes 1572872 | tf_op jit(solution)/shard_map/ppermute | solution.py:402
  100.7 5.0 %collective-permute-start.16 = (bf16[512,128]{1,0:T(8,128)(2,1)S(1)}, bf16[512,128]{1,0:T(8,128)(2,1)S(1)}, u32[]{:S(2)}, u32[]{:S(2)}) collective-permute-start(bf16[512,128]{1,0:T(8,128)(2,1)S(1)} %get-tuple-element.32), channel_id=1, source_target_pairs={{0,16},{4,20},{8,24},{12,28},{16,0},{20,4},{24,8},{28,12},{1,17},{... | collective-permute-start | bytes 393224 | tf_op jit(solution)/shard_map/ppermute | solution.py:323
  101.1 5.0 %collective-permute-start.15 = (bf16[512,128]{1,0:T(8,128)(2,1)S(1)}, bf16[512,128]{1,0:T(8,128)(2,1)S(1)}, u32[]{:S(2)}, u32[]{:S(2)}) collective-permute-start(bf16[512,128]{1,0:T(8,128)(2,1)S(1)} %get-tuple-element.32), channel_id=1, source_target_pairs={{0,8},{4,12},{8,0},{12,4},{16,24},{20,28},{24,16},{28,20},{1,9},{5... | collective-permute-start | bytes 393224 | tf_op jit(solution)/shard_map/ppermute | solution.py:323
  106.7 3.6 %collective-permute-start.18 = (f32[512,128]{1,0:T(8,128)S(1)}, f32[512,128]{1,0:T(8,128)S(1)}, u32[]{:S(2)}, u32[]{:S(2)}) collective-permute-start(f32[512,128]{1,0:T(8,128)S(1)} %shard_map.111.mine), channel_id=1, source_target_pairs={{0,4},{4,0},{8,12},{12,8},{16,20},{20,16},{24,28},{28,24},{1,5},{5... | collective-permute-start | bytes 786440 | tf_op jit(solution)/shard_map/ppermute | solution.py:325
  (3 other events, 3.1 us)
